TPU v7x, 512 devices: a whole 4x8x8 slice. The times are simulated.
512 devices in a mesh: owner: 128 (over y, z, core), rep: 4 (over x).
Axes of the slice: x: 4, y: 8, z: 8, core: 2. Of those that a mesh axis runs over, the one named last changes fastest.
Arguments:
- bin_blocks: int32 [131072], P(('owner', 'rep')), may hold values from 0 to 32767, as said below
- send_counts: int32 [512, 128], P(('owner', 'rep')), may hold values from 0 to 4, as said below
- voxel_index: int32 [131072, 128], P(('owner', 'rep')), may hold values from 0 to 511
- point_sdf: bfloat16 [131072, 128], P(('owner', 'rep')), may hold values from -1 to 1
- point_weight: bfloat16 [131072, 128], P(('owner', 'rep')), may hold values from 0.099609375 to 1
- point_color: bfloat16 [131072, 3, 128], P(('owner', 'rep')), may hold values from 0 to 1
- owner_table: int32 [32768], replicated, may hold values from 0 to 32767, as said below
- old_tsdf: float32 [32768, 4, 512], P(('owner', 'rep')), may hold values from -1 to 1
- old_weight: float32 [32768, 512], P(('owner', 'rep')), may hold values from 0.5 to 4
Outputs:
- new_tsdf: float32 [32768, 4, 512], P(('owner', 'rep'))
- new_weight: float32 [32768, 512], P(('owner', 'rep'))
Inputs may be any that keep to these rules, and one draw needn't show every extreme that they name: `send_counts`: each row sums to 256; every row has an entry equal to 4; among the devices s with the same s mod 4 (one frame group), some owner receives 4 bins from every one of them. `owner_table`: a permutation; entry g is the owner of block g times 256 plus the block's place among that owner's blocks. `bin_blocks`: owner_table assigns the block of bin j of device s to owner p(s, j) of the first step; of the bins that one frame group sends to one owner, at most 128 have places in any one quarter of its 256 places (places q * 64 to (q + 1) * 64 - 1), and this most is reached in every frame group.
All inputs are finite; a program needn't handle non-finite values.
Results may differ from a plain program's by a relative error of at most 0.00078.
Values may be sent and summed in bfloat16 or wider, within the bound.
No kernel may reach another device: no remote copies, remote signals or barrier semaphores. Data moves between devices by JAX's collectives and lax.ppermute only.
A program may use at most 64 MiB of HBM per device.

v0:
```python
import math

import jax
import jax.numpy as jnp
from jax import lax
from jax.sharding import PartitionSpec as P

OWN = 256
VA = 8
VB = 64


def in_one_piece(arrays, axis, split_dim, concat_dim, along):
    widths = [a.shape[along] for a in arrays]
    both = jnp.concatenate(arrays, axis=along)
    filled = lax.all_to_all(both, axis, split_axis=split_dim, concat_axis=concat_dim, tiled=True)
    return tuple(jnp.split(filled, [sum(widths[:k]) for k in range(1, len(widths))], axis=along))


def in_one_piece_2(arrays, axis, split_dim, concat_dim, along):
    widths = [math.prod(a.shape[along:]) for a in arrays]
    both = jnp.concatenate(
        [a.reshape(*a.shape[:along], w) for a, w in zip(arrays, widths)], axis=along
    )
    filled = lax.all_to_all(both, axis, split_axis=split_dim, concat_axis=concat_dim, tiled=True)
    parts = jnp.split(filled, [sum(widths[:k]) for k in range(1, len(widths))], axis=along)
    return tuple(
        (b.reshape(*filled.shape[:along], *a.shape[along:]) for a, b in zip(arrays, parts))
    )


def accumulate(feature_list, voxels, block_rows, block_total):
    slot_count, points = voxels.shape
    group_size = math.gcd(slot_count, 128)
    group_count = slot_count // group_size
    channels = sum_channels(feature_list)
    grouped = tuple((f.reshape((group_count, group_size) + f.shape[1:]) for f in feature_list))
    voxel_groups = voxels.reshape(group_count, group_size, points)
    block_groups = jnp.maximum(block_rows, 0).reshape(group_count, group_size)
    upper_ids = jnp.arange(VA, dtype=jnp.int32)
    lower_ids = jnp.arange(VB, dtype=jnp.int32)

    def fold_group(running, pieces):
        feature_parts, voxel_rows, block_ids = pieces
        features_group = jnp.concatenate(list(feature_parts), axis=1)
        upper_part = voxel_rows // VB
        lower_part = voxel_rows % VB
        chosen = upper_part[:, None, :] == upper_ids[None, :, None]
        left_side = jnp.where(
            chosen[:, None], features_group[:, :, None, :], jnp.zeros((), jnp.bfloat16)
        )
        left_side = left_side.reshape(group_size, channels * VA, points)
        right_side = (lower_part[:, :, None] == lower_ids[None, None, :]).astype(jnp.bfloat16)
        slot_grids = jnp.einsum(
            "gkp,gpb->gkb", left_side, right_side, preferred_element_type=jnp.float32
        )
        slot_grids = slot_grids.reshape(group_size, channels, VA * VB)
        return (running.at[block_ids].add(slot_grids), None)

    running_start = jnp.zeros((block_total, channels, VA * VB), jnp.float32)
    running_end, _ = lax.scan(fold_group, running_start, (grouped, voxel_groups, block_groups))
    return running_end


def sum_channels(feature_list):
    total_channels = 0
    for member in feature_list:
        total_channels = total_channels + member.shape[1]
    return total_channels


def local(
    bin_blocks,
    send_counts,
    voxel_index,
    point_sdf,
    point_weight,
    point_color,
    owner_table,
    old_tsdf,
    old_weight,
):
    owners = lax.axis_size("owner")
    bin_count = bin_blocks.shape[0]
    capacity = 2 * bin_count // owners
    slot_count = owners * capacity
    counts = send_counts[0]
    starts = jnp.cumsum(counts) - counts
    slot_ids = jnp.arange(slot_count, dtype=jnp.int32)
    target = slot_ids // capacity
    position = slot_ids % capacity
    active = position < counts[target]
    source = jnp.clip(starts[target] + position, 0, bin_count - 1)
    blocks_sent = jnp.where(active, owner_table[bin_blocks[source]] % OWN, -1)
    weight = jnp.where(active[:, None], point_weight[source], jnp.zeros((), jnp.bfloat16))
    wide_weight = weight.astype(jnp.float32)
    weighted_sdf = (wide_weight * point_sdf[source].astype(jnp.float32)).astype(jnp.bfloat16)
    geometry = jnp.stack([weight, weighted_sdf], axis=1)
    colors = (wide_weight[:, None, :] * point_color[source].astype(jnp.float32)).astype(
        jnp.bfloat16
    )
    voxels = voxel_index[source]
    replicas = lax.axis_size("rep")
    share = OWN // replicas
    arrived_geometry, arrived_colors, arrived_voxels, arrived_blocks = (
        *in_one_piece((geometry, colors), "owner", 0, 0, 1),
        *in_one_piece_2((voxels, blocks_sent), "owner", 0, 0, 1),
    )
    quota = 2 * bin_count // replicas
    live = arrived_blocks >= 0
    quarter = jnp.where(live, arrived_blocks // share, 0)
    quarter_ids = jnp.arange(replicas, dtype=jnp.int32)
    member = (live[:, None] & (quarter[:, None] == quarter_ids[None, :])).astype(jnp.int32)
    rank = jnp.sum((jnp.cumsum(member, axis=0) - member) * member, axis=1)
    outgoing_slots = replicas * quota
    destination = jnp.where(live, quarter * quota + rank, outgoing_slots).astype(jnp.int32)
    arrived_ids = jnp.arange(arrived_blocks.shape[0], dtype=jnp.int32)
    picked = jnp.zeros((outgoing_slots,), jnp.int32).at[destination].set(arrived_ids, mode="drop")
    filled = jnp.zeros((outgoing_slots,), jnp.bool_).at[destination].set(True, mode="drop")
    send_geometry = jnp.where(
        filled[:, None, None], arrived_geometry[picked], jnp.zeros((), jnp.bfloat16)
    )
    send_colors = jnp.where(
        filled[:, None, None], arrived_colors[picked], jnp.zeros((), jnp.bfloat16)
    )
    send_voxels = arrived_voxels[picked]
    send_places = jnp.where(filled, arrived_blocks[picked] % share, -1).astype(jnp.int32)
    final_geometry, final_colors, final_voxels, final_places = (
        *in_one_piece((send_geometry, send_colors), "rep", 0, 0, 1),
        lax.all_to_all(send_voxels, "rep", split_axis=0, concat_axis=0, tiled=True),
        lax.all_to_all(send_places, "rep", split_axis=0, concat_axis=0, tiled=True),
    )
    cell_sums = accumulate((final_geometry, final_colors), final_voxels, final_places, share)
    geometry_share = cell_sums[:, :2]
    color_share = cell_sums[:, 2:]
    new_weight = old_weight + geometry_share[:, 0]
    joined_sdf = (old_weight * old_tsdf[:, 0] + geometry_share[:, 1]) / new_weight
    joined_color = (old_weight[:, None, :] * old_tsdf[:, 1:] + color_share) / new_weight[:, None, :]
    new_tsdf = jnp.concatenate([joined_sdf[:, None, :], joined_color], axis=1)
    return (new_tsdf, new_weight)


def solution(mesh):
    placed = (
        P(("owner", "rep")),
        P(("owner", "rep"), None),
        P(("owner", "rep"), None),
        P(("owner", "rep"), None),
        P(("owner", "rep"), None),
        P(("owner", "rep"), None, None),
        P(),
        P(("owner", "rep"), None, None),
        P(("owner", "rep"), None),
    )
    return jax.shard_map(
        local,
        mesh=mesh,
        in_specs=placed,
        out_specs=(P(("owner", "rep"), None, None), P(("owner", "rep"), None)),
        check_vma=False,
    )
```

profile of v0, /device:TPU:6, one launch (start us, length us, event | category | flops | bytes accessed | tf_op | source)
XLA Modules:
  0.0 210.6 jit_solution(4263161496959832340)
XLA Ops:
  2.4 3.3 %gather_fusion = s32[512]{0:T(512)S(1)} fusion(s32[128]{0:T(128)S(1)} %bitcast_subtract_fusion, s32[1024]{0:T(1024)S(1)} %pad_clamp_fusion.3), kind=kCustom, calls=%fused_computation | custom fusion | bytes 6144 | tf_op jit(solution)/shard_map/gather | solution.py:93
  5.8 3.5 %gather_fusion.3 = s32[512]{0:T(512)S(1)} fusion(s32[256]{0:T(256)S(1)} %copy-done.2, s32[1024]{0:T(1024)S(1)} %pad_clamp_fusion.2), kind=kCustom, calls=%fused_computation.3 | custom fusion | bytes 6144 | tf_op jit(solution)/shard_map/gather | solution.py:94
  9.4 3.1 %gather_fusion.4 = s32[512]{0:T(512)S(1)} fusion(s32[32768]{0:T(1024)S(1)} %copy-done.3, s32[1024]{0:T(1024)S(1)} %pad_clamp_fusion.1), kind=kCustom, calls=%fused_computation.4 | custom fusion | bytes 6144 | tf_op jit(solution)/shard_map/gather | solution.py:94
  12.7 3.3 %gather_fusion.2 = s32[512]{0:T(512)S(1)} fusion(s32[128]{0:T(128)S(1)} %bitcast.122, s32[1024]{0:T(1024)S(1)} %pad_clamp_fusion.3), kind=kCustom, calls=%fused_computation.2 | custom fusion | bytes 6144 | tf_op jit(solution)/shard_map/gather | solution.py:92
  17.1 1.0 gather_fusion.1
  19.1 17.8 %all-to-all-start = ((s32[128,4,129]{2,1,0:T(4,128)}), s32[128,4,129]{2,1,0:T(4,128)S(1)}, u32[]{:S(2)}, u32[]{:S(2)}) async-start(s32[128,4,129]{2,1,0:T(4,128)} %pad_add_fusion), calls=%async_computation | async-start | bytes 1048576 | tf_op jit(solution)/shard_map/all_to_all | solution.py:25
  36.9 1.3 gather_fusion.7
  38.3 1.3 gather_fusion.8
  39.6 2.7 %gather_fusion.9 = bf16[512,3,128]{2,0,1:T(8,128)(2,1)S(1)} fusion(bf16[256,3,128]{2,0,1:T(8,128)(2,1)S(1)} %copy-done, s32[1024]{0:T(1024)S(1)} %pad_clamp_fusion.2), kind=kCustom, calls=%fused_computation.9 | custom fusion | bytes 788480 | tf_op jit(solution)/shard_map/gather | solution.py:99
  42.8 1.5 copy.45
  44.3 13.2 %all-to-all-done = s32[128,4,129]{2,1,0:T(4,128)S(1)} async-done(((s32[128,4,129]{2,1,0:T(4,128)}), s32[128,4,129]{2,1,0:T(4,128)S(1)}, u32[]{:S(2)}, u32[]{:S(2)}) %all-to-all-start) | async-done | bytes 264224 | tf_op jit(solution)/shard_map/all_to_all | solution.py:25
  57.5 6.2 %all-to-all-start.3 = ((bf16[512,5,128]{2,1,0:T(8,128)(2,1)}), bf16[512,5,128]{2,1,0:T(8,128)(2,1)S(1)}, u32[]{:S(2)}, u32[]{:S(2)}) async-start(bf16[512,5,128]{2,1,0:T(8,128)(2,1)} %copy.45), calls=%async_computation.3 | async-start | bytes 2097152 | tf_op jit(solution)/shard_map/all_to_all | solution.py:16
  64.1 1.2 reduce-window.20
  65.9 2.6 %scatter_custom_fusion.2 = s32[512]{0:T(512)S(1)} fusion(s32[512]{0:T(512)S(1)} %bitcast.136, s32[512]{0:T(512)S(1)} %iota.48, s32[]{:T(128)} %copy.70), kind=kCustom, calls=%fused_computation.118 | custom fusion | bytes 2052 | tf_op jit(solution)/shard_map/scatter | solution.py:118
  68.5 2.4 %scatter_custom_fusion.1 = pred[512]{0:T(512)(128)(4,1)S(1)} fusion(s32[512]{0:T(512)S(1)} %bitcast.137, pred[512]{0:T(512)(128)(4,1)S(1)} %broadcast.498, pred[]{:T(512)} %constant.145.clone.1), kind=kCustom, calls=%fused_computation.122 | custom fusion | bytes 513 | tf_op jit(solution)/shard_map/scatter | solution.py:119
  71.0 3.5 %gather_fusion.5 = s32[512]{0:T(512)S(1)} fusion(s32[512]{0:T(512)S(1)} %bitcast.123, s32[1024]{0:T(1024)S(1)} %pad_clamp_fusion), kind=kCustom, calls=%fused_computation.5 | custom fusion | bytes 6144 | tf_op jit(solution)/shard_map/gather | solution.py:127
  75.1 19.7 %all-to-all-done.3 = bf16[512,5,128]{2,1,0:T(8,128)(2,1)S(1)} async-done(((bf16[512,5,128]{2,1,0:T(8,128)(2,1)}), bf16[512,5,128]{2,1,0:T(8,128)(2,1)S(1)}, u32[]{:S(2)}, u32[]{:S(2)}) %all-to-all-start.3) | async-done | bytes 655392 | tf_op jit(solution)/shard_map/all_to_all | solution.py:16
  94.8 4.8 %all-to-all-start.1 = ((s32[4,128,1]{1,2,0:T(1,128)}), s32[4,128,1]{1,2,0:T(1,128)S(1)}, u32[]{:S(2)}, u32[]{:S(2)}) async-start(s32[4,128,1]{1,2,0:T(1,128)} %bitcast.15), calls=%async_computation.1 | async-start | bytes 4096 | tf_op jit(solution)/shard_map/all_to_all | solution.py:131
  99.7 2.1 %gather_fusion.10 = bf16[512,2,128]{2,1,0:T(2,128)(2,1)S(1)} fusion(bf16[512,2,128]{2,1,0:T(2,128)(2,1)S(1)} %split.26, s32[1024]{0:T(1024)S(1)} %pad_clamp_fusion), kind=kCustom, calls=%fused_computation.10 | custom fusion | bytes 526336 | tf_op jit(solution)/shard_map/gather | solution.py:121
  101.9 1.8 broadcast_select_fusion.1
  103.9 2.1 gather_fusion.11
  106.0 1.8 broadcast_select_fusion
  107.8 1.5 pad_maximum_fusion.1
  109.3 4.8 %all-to-all-start.4 = ((bf16[512,5,128]{2,1,0:T(8,128)(2,1)}), bf16[512,5,128]{2,1,0:T(8,128)(2,1)S(1)}, u32[]{:S(2)}, u32[]{:S(2)}) async-start(bf16[512,5,128]{2,1,0:T(8,128)(2,1)} %pad_maximum_fusion.1), calls=%async_computation.4 | async-start | bytes 2097152 | tf_op jit(solution)/shard_map/all_to_all | solution.py:16
  114.1 1.6 gather_fusion.6
  115.8 9.8 %all-to-all-done.4 = bf16[512,5,128]{2,1,0:T(8,128)(2,1)S(1)} async-done(((bf16[512,5,128]{2,1,0:T(8,128)(2,1)}), bf16[512,5,128]{2,1,0:T(8,128)(2,1)S(1)}, u32[]{:S(2)}, u32[]{:S(2)}) %all-to-all-start.4) | async-done | bytes 655392 | tf_op jit(solution)/shard_map/all_to_all | solution.py:16
  125.6 6.1 %all-to-all-start.2 = ((s32[4,128,128]{2,1,0:T(8,128)}), s32[4,128,128]{2,1,0:T(8,128)}, u32[]{:S(2)}, u32[]{:S(2)}) async-start(s32[4,128,128]{2,1,0:T(8,128)} %bitcast.17), calls=%async_computation.2 | async-start | bytes 524288 | tf_op jit(solution)/shard_map/all_to_all | solution.py:130
  131.6 1.1 split.29
  133.6 2.8 %all-to-all-done.2 = s32[4,128,128]{2,1,0:T(8,128)} async-done(((s32[4,128,128]{2,1,0:T(8,128)}), s32[4,128,128]{2,1,0:T(8,128)}, u32[]{:S(2)}, u32[]{:S(2)}) %all-to-all-start.2) | async-done | bytes 262176 | tf_op jit(solution)/shard_map/all_to_all | solution.py:130
  136.5 71.1 %while.13 = (s32[]{:T(128)}, f32[64,5,512]{2,1,0:T(8,128)S(1)}, s32[4,128]{1,0:T(4,128)S(1)}, s32[4,128,128]{2,1,0:T(8,128)}, bf16[4,128,2,128]{3,2,1,0:T(2,128)...) while((s32[]{:T(128)}, f32[64,5,512]{2,1,0:T(8,128)S(1)}, s32[4,128]{1,0:T(4,128)S(1)}, ...), condition=%wide.region_8.9_spmd.clone, body=%wide.region_6.8_spmd.clone.sunk | while | flops 86786432 | bytes 11994721 | solution.py:61
  138.3 1.0 dynamic-slice_bitcast_fusion.4
  140.4 2.8 %fusion.53 = f32[128,40,64]{2,1,0:T(8,128)} fusion(s32[128,128]{1,0:T(8,128)S(1)} %add_select_fusion.9, pred[128,8,128]{2,1,0:T(8,128)(4,1)S(1)} %iota_compare_fusion.8, bf16[128,5,128]{2,1,0:T(8,128)(2,1)S(1)} %pad_maximum_fusion.5), kind=kOutput, calls=%fused_computation.18.clone.1 | convolution fusion | flops 85590016 | bytes 1671168 | tf_op jit(solution)/shard_map/while/body/eval_jaxpr/gkp,gpb->gkb/dot_general | solution.py:54
  143.1 3.2 %copy.60 = f32[128,40,64]{0,2,1:T(8,128)} copy(f32[128,40,64]{2,1,0:T(8,128)} %fusion.53) | data formatting | bytes 2621440 | tf_op jit(solution)/shard_map/while/body/eval_jaxpr/gkp,gpb->gkb/dot_general | solution.py:54
  146.3 2.1 %copy.61 = f32[128,5,512]{2,1,0:T(8,128)S(1)} copy(f32[128,5,512]{0,2,1:T(8,128)} %bitcast.124) | data formatting | bytes 2621440 | tf_op jit(solution)/shard_map/while/body/eval_jaxpr/reshape | solution.py:57
  148.4 5.8 %scatter_fusion = f32[64,5,512]{2,1,0:T(8,128)S(1)} fusion(f32[64,5,512]{2,1,0:T(8,128)S(1)} %get-tuple-element.189, s32[128]{0:T(128)S(1)} %fusion.52, f32[128,5,512]{2,1,0:T(8,128)S(1)} %copy.61), kind=kCustom, calls=%fused_computation.12.clone.clone.1 | custom fusion | flops 327680 | bytes 3932672 | tf_op jit(solution)/shard_map/while/body/eval_jaxpr/scatter-add | solution.py:58
  158.2 2.8 %fusion.53 = f32[128,40,64]{2,1,0:T(8,128)} fusion(s32[128,128]{1,0:T(8,128)S(1)} %add_select_fusion.9, pred[128,8,128]{2,1,0:T(8,128)(4,1)S(1)} %iota_compare_fusion.8, bf16[128,5,128]{2,1,0:T(8,128)(2,1)S(1)} %pad_maximum_fusion.5), kind=kOutput, calls=%fused_computation.18.clone.1 | convolution fusion | flops 85590016 | bytes 1671168 | tf_op jit(solution)/shard_map/while/body/eval_jaxpr/gkp,gpb->gkb/dot_general | solution.py:54
  160.9 3.2 %copy.60 = f32[128,40,64]{0,2,1:T(8,128)} copy(f32[128,40,64]{2,1,0:T(8,128)} %fusion.53) | data formatting | bytes 2621440 | tf_op jit(solution)/shard_map/while/body/eval_jaxpr/gkp,gpb->gkb/dot_general | solution.py:54
  164.1 2.1 %copy.61 = f32[128,5,512]{2,1,0:T(8,128)S(1)} copy(f32[128,5,512]{0,2,1:T(8,128)} %bitcast.124) | data formatting | bytes 2621440 | tf_op jit(solution)/shard_map/while/body/eval_jaxpr/reshape | solution.py:57
  166.2 5.8 %scatter_fusion = f32[64,5,512]{2,1,0:T(8,128)S(1)} fusion(f32[64,5,512]{2,1,0:T(8,128)S(1)} %get-tuple-element.189, s32[128]{0:T(128)S(1)} %fusion.52, f32[128,5,512]{2,1,0:T(8,128)S(1)} %copy.61), kind=kCustom, calls=%fused_computation.12.clone.clone.1 | custom fusion | flops 327680 | bytes 3932672 | tf_op jit(solution)/shard_map/while/body/eval_jaxpr/scatter-add | solution.py:58
  176.0 2.8 %fusion.53 = f32[128,40,64]{2,1,0:T(8,128)} fusion(s32[128,128]{1,0:T(8,128)S(1)} %add_select_fusion.9, pred[128,8,128]{2,1,0:T(8,128)(4,1)S(1)} %iota_compare_fusion.8, bf16[128,5,128]{2,1,0:T(8,128)(2,1)S(1)} %pad_maximum_fusion.5), kind=kOutput, calls=%fused_computation.18.clone.1 | convolution fusion | flops 85590016 | bytes 1671168 | tf_op jit(solution)/shard_map/while/body/eval_jaxpr/gkp,gpb->gkb/dot_general | solution.py:54
  178.7 3.2 %copy.60 = f32[128,40,64]{0,2,1:T(8,128)} copy(f32[128,40,64]{2,1,0:T(8,128)} %fusion.53) | data formatting | bytes 2621440 | tf_op jit(solution)/shard_map/while/body/eval_jaxpr/gkp,gpb->gkb/dot_general | solution.py:54
  181.9 2.1 %copy.61 = f32[128,5,512]{2,1,0:T(8,128)S(1)} copy(f32[128,5,512]{0,2,1:T(8,128)} %bitcast.124) | data formatting | bytes 2621440 | tf_op jit(solution)/shard_map/while/body/eval_jaxpr/reshape | solution.py:57
  184.0 5.8 %scatter_fusion = f32[64,5,512]{2,1,0:T(8,128)S(1)} fusion(f32[64,5,512]{2,1,0:T(8,128)S(1)} %get-tuple-element.189, s32[128]{0:T(128)S(1)} %fusion.52, f32[128,5,512]{2,1,0:T(8,128)S(1)} %copy.61), kind=kCustom, calls=%fused_computation.12.clone.clone.1 | custom fusion | flops 327680 | bytes 3932672 | tf_op jit(solution)/shard_map/while/body/eval_jaxpr/scatter-add | solution.py:58
  193.7 2.8 %fusion.53 = f32[128,40,64]{2,1,0:T(8,128)} fusion(s32[128,128]{1,0:T(8,128)S(1)} %add_select_fusion.9, pred[128,8,128]{2,1,0:T(8,128)(4,1)S(1)} %iota_compare_fusion.8, bf16[128,5,128]{2,1,0:T(8,128)(2,1)S(1)} %pad_maximum_fusion.5), kind=kOutput, calls=%fused_computation.18.clone.1 | convolution fusion | flops 85590016 | bytes 1671168 | tf_op jit(solution)/shard_map/while/body/eval_jaxpr/gkp,gpb->gkb/dot_general | solution.py:54
  196.5 3.2 %copy.60 = f32[128,40,64]{0,2,1:T(8,128)} copy(f32[128,40,64]{2,1,0:T(8,128)} %fusion.53) | data formatting | bytes 2621440 | tf_op jit(solution)/shard_map/while/body/eval_jaxpr/gkp,gpb->gkb/dot_general | solution.py:54
  199.6 2.1 %copy.61 = f32[128,5,512]{2,1,0:T(8,128)S(1)} copy(f32[128,5,512]{0,2,1:T(8,128)} %bitcast.124) | data formatting | bytes 2621440 | tf_op jit(solution)/shard_map/while/body/eval_jaxpr/reshape | solution.py:57
  201.8 5.8 %scatter_fusion = f32[64,5,512]{2,1,0:T(8,128)S(1)} fusion(f32[64,5,512]{2,1,0:T(8,128)S(1)} %get-tuple-element.189, s32[128]{0:T(128)S(1)} %fusion.52, f32[128,5,512]{2,1,0:T(8,128)S(1)} %copy.61), kind=kCustom, calls=%fused_computation.12.clone.clone.1 | custom fusion | flops 327680 | bytes 3932672 | tf_op jit(solution)/shard_map/while/body/eval_jaxpr/scatter-add | solution.py:58
  209.5 1.0 pad_maximum_fusion.3
  (96 shorter events, 23.6 us)
Async XLA Ops:
  0.6 39.0 %copy-start = (bf16[256,3,128]{2,0,1:T(8,128)(2,1)S(1)}, bf16[256,3,128]{2,0,1:T(8,128)(2,1)}, u32[]{:S(2)}) copy-start(bf16[256,3,128]{2,0,1:T(8,128)(2,1)} %param.16) | copy-start | bytes 589828
  0.6 5.2 %copy-start.2 = (s32[256]{0:T(256)S(1)}, s32[256]{0:T(256)}, u32[]{:S(2)}) copy-start(s32[256]{0:T(256)} %param.11) | copy-start | bytes 3076
  2.4 7.0 %copy-start.3 = (s32[32768]{0:T(1024)S(1)}, s32[32768]{0:T(1024)}, u32[]{:S(2)}) copy-start(s32[32768]{0:T(1024)} %param.17) | copy-start | bytes 393220
  5.8 6.8 %copy-start.1 = (s32[1,128]{1,0:T(1,128)S(1)}, s32[1,128]{1,0:T(1,128)}, u32[]{:S(2)}) copy-start(s32[1,128]{1,0:T(1,128)} %param.12) | copy-start | bytes 1540
  9.4 7.7 %copy-start.4 = (s32[256,128]{1,0:T(8,128)S(1)}, s32[256,128]{1,0:T(8,128)}, u32[]{:S(2)}) copy-start(s32[256,128]{1,0:T(8,128)} %param.13) | copy-start | bytes 393220
  17.1 19.8 %copy-start.5 = (bf16[256,128]{1,0:T(8,128)(2,1)S(1)}, bf16[256,128]{1,0:T(8,128)(2,1)}, u32[]{:S(2)}) copy-start(bf16[256,128]{1,0:T(8,128)(2,1)} %param.15) | copy-start | bytes 196612
  18.1 20.1 %copy-start.6 = (bf16[256,128]{1,0:T(8,128)(2,1)S(1)}, bf16[256,128]{1,0:T(8,128)(2,1)}, u32[]{:S(2)}) copy-start(bf16[256,128]{1,0:T(8,128)(2,1)} %param.14) | copy-start | bytes 196612
  19.1 38.5 %all-to-all-start = ((s32[128,4,129]{2,1,0:T(4,128)}), s32[128,4,129]{2,1,0:T(4,128)S(1)}, u32[]{:S(2)}, u32[]{:S(2)}) async-start(s32[128,4,129]{2,1,0:T(4,128)} %pad_add_fusion), calls=%async_computation | async-start | bytes 1048576 | tf_op jit(solution)/shard_map/all_to_all | solution.py:25
  57.5 37.3 %all-to-all-start.3 = ((bf16[512,5,128]{2,1,0:T(8,128)(2,1)}), bf16[512,5,128]{2,1,0:T(8,128)(2,1)S(1)}, u32[]{:S(2)}, u32[]{:S(2)}) async-start(bf16[512,5,128]{2,1,0:T(8,128)(2,1)} %copy.45), calls=%async_computation.3 | async-start | bytes 2097152 | tf_op jit(solution)/shard_map/all_to_all | solution.py:16
  94.8 14.5 %all-to-all-start.1 = ((s32[4,128,1]{1,2,0:T(1,128)}), s32[4,128,1]{1,2,0:T(1,128)S(1)}, u32[]{:S(2)}, u32[]{:S(2)}) async-start(s32[4,128,1]{1,2,0:T(1,128)} %bitcast.15), calls=%async_computation.1 | async-start | bytes 4096 | tf_op jit(solution)/shard_map/all_to_all | solution.py:131
  109.3 16.3 %all-to-all-start.4 = ((bf16[512,5,128]{2,1,0:T(8,128)(2,1)}), bf16[512,5,128]{2,1,0:T(8,128)(2,1)S(1)}, u32[]{:S(2)}, u32[]{:S(2)}) async-start(bf16[512,5,128]{2,1,0:T(8,128)(2,1)} %pad_maximum_fusion.1), calls=%async_computation.4 | async-start | bytes 2097152 | tf_op jit(solution)/shard_map/all_to_all | solution.py:16
  125.6 10.8 %all-to-all-start.2 = ((s32[4,128,128]{2,1,0:T(8,128)}), s32[4,128,128]{2,1,0:T(8,128)}, u32[]{:S(2)}, u32[]{:S(2)}) async-start(s32[4,128,128]{2,1,0:T(8,128)} %bitcast.17), calls=%async_computation.2 | async-start | bytes 524288 | tf_op jit(solution)/shard_map/all_to_all | solution.py:130
  136.5 71.6 %slice-start = ((f32[64,4,512]{2,1,0:T(4,128)}), f32[64,1,512]{2,1,0:T(1,128)S(1)}, s32[]{:S(2)}) async-start(f32[64,4,512]{2,1,0:T(4,128)} %param.18), calls=%async_computation.5 | async-start | bytes 262144 | tf_op jit(solution)/shard_map/slice | solution.py:137
  207.6 1.4 copy-start.7
  207.6 1.4 copy-start.8
  209.0 1.6 copy-start.9
where the time goes:
time: 213 us; the launch traced here: 211 us
  local copies, waits for them, and re-layouts  69.7 us (33%)
  waiting for transfers between devices  45.5 us (21%)
  other arithmetic  43.3 us (20%)
  starting transfers between devices  39.6 us (19%)
  matrix products  11 us (5%)
    all_to_all x2, waiting for transfers between devices, in_one_piece(): lax.all_to_all(both, axis, split_axis=split_dim, concat_axis=concat_dim,...  29.5 us
    scatter-add x4, other arithmetic, fold_group(): return (running.at[block_ids].add(slot_grids), None)  23.3 us
    all_to_all x1, starting transfers between devices, in_one_piece_2(): lax.all_to_all(both, axis, split_axis=split_dim, concat_axis=concat_dim,...  17.8 us
    all_to_all x1, waiting for transfers between devices, in_one_piece_2(): lax.all_to_all(both, axis, split_axis=split_dim, concat_axis=concat_dim,...  13.2 us
    dot_general x4, local copies, waits for them, and re-layouts, fold_group(): jnp.einsum('gkp,gpb->gkb', left_side, right_side, preferred_element_type=...  12.6 us
    dot_general x4, matrix products, fold_group(): jnp.einsum('gkp,gpb->gkb', left_side, right_side, preferred_element_type=...  11 us
    all_to_all x2, starting transfers between devices, in_one_piece(): lax.all_to_all(both, axis, split_axis=split_dim, concat_axis=concat_dim,...  11 us
    reshape x4, local copies, waits for them, and re-layouts, fold_group(): slot_grids = slot_grids.reshape(group_size, channels, VA * VB)  8.49 us
  transfers between devices with their start and end apart: 5, of which 4 were waited for; matrix products, arithmetic and copies ran while one was open for 15% of the time, Pallas kernels for 0%

commit v1 on v0

v1 whole, which is shorter than its diff:
```python
import functools
import jax, jax.numpy as jnp
from jax import lax
from jax.experimental import pallas as pl
from jax.experimental.pallas import tpu as pltpu
from jax.sharding import PartitionSpec as P
bf16=jnp.bfloat16; f32=jnp.float32; i32=jnp.int32
OWN=256
def row_ids(shape,dim): return lax.broadcasted_iota(i32,shape,dim)

def pack_kernel(counts_ref, blocks_ref, table_ref, voxel_ref, sdf_ref, weight_ref, color_ref, out_ref):
    owners=counts_ref.shape[1]; bins=blocks_ref.shape[1]
    counts=jnp.broadcast_to(counts_ref[...],(owners,owners)).astype(f32)
    up=row_ids((owners,owners),0); across=row_ids((owners,owners),1)
    ends=jnp.sum(jnp.where(across<=up,counts,0.0),axis=1,keepdims=True)
    own=jnp.sum(jnp.where(across==up,counts,0.0),axis=1,keepdims=True)
    bin_ids=row_ids((owners,bins),1).astype(f32)
    passed=bin_ids>=ends
    target=jnp.sum(jnp.where(passed,1.0,0.0),axis=0,keepdims=True)
    before=jnp.sum(jnp.where(passed,own,0.0),axis=0,keepdims=True)
    slot=(8.0*target+bin_ids[:1]-before).astype(i32)
    blocks=blocks_ref[...]
    trows=table_ref.shape[0]
    pick=jnp.where(row_ids((trows,bins),0)==blocks//128,1.0,0.0).astype(bf16)
    table=(table_ref[...]%OWN).astype(f32).astype(bf16)
    found=lax.dot_general(table,pick,(((0,),(0,)),((),())),preferred_element_type=f32)
    place=jnp.sum(jnp.where(row_ids((128,bins),0)==blocks%128,found,0.0),axis=0,keepdims=True)+1.0
    select=jnp.where(row_ids((8*owners,bins),0)==slot,1.0,0.0).astype(bf16)
    def put(c,values):
        out_ref[:,:,c*128:(c+1)*128]=values.reshape(owners,8,128)[:,:4].astype(bf16)
    weight=weight_ref[...].astype(f32)
    feats=[(voxel_ref[...]-256).astype(f32).astype(bf16),weight_ref[...],(weight*sdf_ref[...].astype(f32)).astype(bf16)]
    feats+=[(weight*color_ref[c].astype(f32)).astype(bf16) for c in range(3)]
    for c in range(0,6,2):
        got=jnp.dot(select,jnp.concatenate(feats[c:c+2],axis=1),preferred_element_type=f32)
        put(c,got[:,:128]); put(c+1,got[:,128:])
    put(6,lax.dot_general(select,jnp.broadcast_to(place,(128,bins)).astype(bf16),(((1,),(1,)),((),())),preferred_element_type=f32))

def pack(counts,blocks,table,voxel,sdf,weight,color):
    owners=counts.shape[1]
    return pl.pallas_call(pack_kernel,out_shape=jax.ShapeDtypeStruct((owners,4,7*128),bf16),
        compiler_params=pltpu.CompilerParams(vmem_limit_bytes=48<<20),name="pack")(counts,blocks.reshape(1,-1),table.reshape(-1,128),voxel,sdf,weight,color.transpose(1,0,2))

def rows_of(ref,c):
    x=ref[:,:,c*128:(c+1)*128]
    return x.reshape(4*x.shape[0],128)

def route_kernel(replicas,in_ref,out_ref):
    quota=out_ref.shape[0]//replicas
    share=OWN//replicas
    codes=rows_of(in_ref,6)
    n=codes.shape[0]
    eye=jnp.where(row_ids((128,128),0)==row_ids((128,128),1),1.0,0.0)
    lower=jnp.where(row_ids((128,128),0)<row_ids((128,128),1),1.0,0.0).astype(bf16)
    quarters=row_ids((8,128),0).astype(f32)
    total=jnp.zeros((8,1),f32)
    dests=[]
    for g in range(n//128):
        code=jnp.sum(codes[g*128:(g+1)*128].astype(f32)*eye,axis=0,keepdims=True)
        live=code>0.5
        quarter=jnp.where(live,jnp.floor((code-1.0)*(1.0/share)),9.0)
        member=jnp.where(quarters==quarter,1.0,0.0)
        ahead=jnp.dot(member.astype(bf16),lower,preferred_element_type=f32)+total
        total=total+jnp.sum(member,axis=1,keepdims=True)
        rank=jnp.sum(ahead*member,axis=0,keepdims=True)
        dests.append(jnp.where(live,quarter*quota+rank,-1.0))
    dest=jnp.concatenate(dests,axis=1).astype(i32)
    select=jnp.where(row_ids((replicas*quota,n),0)==dest,1.0,0.0).astype(bf16)
    for c in range(0,7,2):
        w=min(2,7-c)
        x=jnp.concatenate([rows_of(in_ref,c+k) for k in range(w)],axis=1)
        out_ref[:,c*128:(c+w)*128]=jnp.dot(select,x,preferred_element_type=f32).astype(bf16)

def route(x,replicas):
    bins=x.shape[0]*2
    quota=2*bins//replicas
    return pl.pallas_call(functools.partial(route_kernel,replicas),out_shape=jax.ShapeDtypeStruct((replicas*quota,7*128),bf16),
        compiler_params=pltpu.CompilerParams(vmem_limit_bytes=48<<20),name="route")(x)

GROUP=16
def join_kernel(pair,in_ref,tsdf_ref,weight_ref,new_tsdf_ref,new_weight_ref,acc_ref,codes_ref,code_smem,sem):
    rows=in_ref.shape[0]; places=weight_ref.shape[0]
    share=places
    sources=rows//128
    acc_ref[...]=jnp.zeros_like(acc_ref)
    eye=jnp.where(row_ids((128,128),0)==row_ids((128,128),1),1.0,0.0)
    for r in range(sources):
        code=jnp.sum(in_ref[r*128:(r+1)*128,6*128:7*128].astype(f32)*eye,axis=0,keepdims=True)
        spot=code-1.0
        spot=spot-jnp.floor(spot*(1.0/share))*share
        codes_ref[r:r+1,:]=jnp.where(code>0.5,spot,0.0).astype(i32)
        live=jnp.sum(jnp.where(code>0.5,1.0,0.0),axis=1,keepdims=True)
        codes_ref[sources+r:sources+r+1,:]=jnp.broadcast_to(live,(1,128)).astype(i32)
    copy=pltpu.make_async_copy(codes_ref,code_smem,sem); copy.start(); copy.wait()
    lanes=row_ids((128,128),0).astype(f32).astype(bf16)
    sub=row_ids((8,128),0)
    def group(r,base):
        start=pl.multiple_of(r*128+base*GROUP,GROUP)
        tiles=[in_ref[pl.ds(start,GROUP),c*128:(c+1)*128].astype(f32) for c in range(6)]
        voxel=tiles[0]+256.0
        upper=jnp.floor(voxel*(1.0/128.0)); lower=(voxel-upper*128.0).astype(bf16)
        def parts(b):
            hot=jnp.where(lanes==jnp.broadcast_to(lower[b:b+1],(128,128)),jnp.ones((),bf16),jnp.zeros((),bf16))
            feat=jnp.zeros((8,128),f32)
            for c in range(5): feat=jnp.where(sub==c,jnp.broadcast_to(tiles[1+c][b:b+1],(8,128)),feat)
            up=jnp.broadcast_to(upper[b:b+1],(8,128))
            left=jnp.concatenate([jnp.where(up==a,feat,0.0) for a in range(4)],axis=0).astype(bf16)
            return hot,left
        def add(b,grid):
            place=code_smem[r,base*GROUP+b]
            at=pl.ds(pl.multiple_of(place*32,32),32)
            acc_ref[at,:]+=grid
        if pair==1:
            for b in range(GROUP):
                hot,left=parts(b)
                add(b,lax.dot_general(left,hot,(((1,),(1,)),((),())),preferred_element_type=f32))
        else:
            for b in range(0,GROUP,2):
                h0,l0=parts(b); h1,l1=parts(b+1)
                z=jnp.zeros_like(l0)
                left=jnp.concatenate([jnp.concatenate([l0,z],axis=1),jnp.concatenate([z,l1],axis=1)],axis=0)
                g=lax.dot_general(left,jnp.concatenate([h0,h1],axis=1),(((1,),(1,)),((),())),preferred_element_type=f32)
                add(b,g[:32]); add(b+1,g[32:])
    for r in range(sources):
        n=(code_smem[sources+r,0]+GROUP-1)//GROUP
        def body(base,carry):
            group(r,base); return carry
        lax.fori_loop(0,n,body,0)
    for a in range(4):
        cols=slice(a*128,(a+1)*128)
        old=weight_ref[:,cols]
        new=old+acc_ref[pl.ds(a*8,places,stride=32),:]
        new_weight_ref[:,cols]=new
        for c in range(4):
            new_tsdf_ref[:,c,cols]=(old*tsdf_ref[:,c,cols]+acc_ref[pl.ds(a*8+1+c,places,stride=32),:])/new

def join(x,old_tsdf,old_weight,pair=2):
    places=old_weight.shape[0]; sources=x.shape[0]//128
    return pl.pallas_call(functools.partial(join_kernel,pair),
        out_shape=(jax.ShapeDtypeStruct(old_tsdf.shape,f32),jax.ShapeDtypeStruct(old_weight.shape,f32)),
        scratch_shapes=[pltpu.VMEM((places*32,128),f32),pltpu.VMEM((2*sources,128),i32),pltpu.SMEM((2*sources,128),i32),pltpu.SemaphoreType.DMA(())],
        compiler_params=pltpu.CompilerParams(vmem_limit_bytes=48<<20),name="join")(x,old_tsdf,old_weight)


def local(bin_blocks,send_counts,voxel_index,point_sdf,point_weight,point_color,owner_table,old_tsdf,old_weight):
    packed=pack(send_counts,bin_blocks,owner_table,voxel_index,point_sdf,point_weight,point_color)
    arrived=lax.all_to_all(packed,"owner",split_axis=0,concat_axis=0,tiled=True)
    sent=route(arrived,lax.axis_size("rep"))
    final=lax.all_to_all(sent,"rep",split_axis=0,concat_axis=0,tiled=True)
    return join(final,old_tsdf,old_weight)


def solution(mesh):
    both=("owner","rep")
    placed=(P(both),P(both,None),P(both,None),P(both,None),P(both,None),P(both,None,None),P(),P(both,None,None),P(both,None))
    return jax.shard_map(local,mesh=mesh,in_specs=placed,out_specs=(P(both,None,None),P(both,None)),check_vma=False)
```

time: 213 us -> 79 us (0.37)
  the two profiles are of different devices: /device:TPU:6 before, /device:TPU:24 now
where the time goes in v1:
time: 79 us; the launch traced here: 78.6 us
  blocking collectives  62.2 us (79%)
  Pallas kernels  10.6 us (13%)
  local copies, waits for them, and re-layouts  5.09 us (6%)
    all_to_all x1, blocking collectives, local(): lax.all_to_all(packed, 'owner', split_axis=0, concat_axis=0, tiled=True)  43.2 us
    all_to_all x1, blocking collectives, local(): final = lax.all_to_all(sent, 'rep', split_axis=0, concat_axis=0, tiled=True)  19.1 us
    pallas_call x1, Pallas kernels, join(): pl.pallas_call(functools.partial(join_kernel, pair), out_shape=(jax.Shape...  8.93 us
    unnamed x18, local copies, waits for them, and re-layouts  5.09 us

profile of v1, /device:TPU:24, one launch (start us, length us, event | category | flops | bytes accessed | tf_op | source)
XLA Modules:
  0.0 78.6 jit_solution(6391696055555895562)
XLA Ops:
  0.6 0.0 copy-start.7
  0.6 0.0 copy-start.8
  0.7 0.7 copy-done.7
  1.3 0.0 copy-done.8
  1.3 0.0 copy-start.1
  1.3 0.9 %copy-done.1 = bf16[256,3,128]{2,0,1:T(8,128)(2,1)S(1)} copy-done((bf16[256,3,128]{2,0,1:T(8,128)(2,1)S(1)}, bf16[256,3,128]{2,0,1:T(8,128)(2,1)}, u32[]{:S(2)}) %copy-start.1) | copy-done | bytes 196632
  2.2 0.0 copy-start.2
  2.2 0.9 %copy-done.2 = s32[32768]{0:T(1024)S(1)} copy-done((s32[32768]{0:T(1024)S(1)}, s32[32768]{0:T(1024)}, u32[]{:S(2)}) %copy-start.2) | copy-done | bytes 131096
  3.1 0.0 copy-start.3
  3.1 0.9 %copy-done.3 = s32[256,128]{1,0:T(8,128)S(1)} copy-done((s32[256,128]{1,0:T(8,128)S(1)}, s32[256,128]{1,0:T(8,128)}, u32[]{:S(2)}) %copy-start.3) | copy-done | bytes 131096
  4.1 0.0 copy-start.5
  4.1 0.8 %copy-done.5 = bf16[256,128]{1,0:T(8,128)(2,1)S(1)} copy-done((bf16[256,128]{1,0:T(8,128)(2,1)S(1)}, bf16[256,128]{1,0:T(8,128)(2,1)}, u32[]{:S(2)}) %copy-start.5) | copy-done | bytes 65560
  4.9 0.0 copy-start.6
  4.9 0.8 %copy-done.6 = bf16[256,128]{1,0:T(8,128)(2,1)S(1)} copy-done((bf16[256,128]{1,0:T(8,128)(2,1)S(1)}, bf16[256,128]{1,0:T(8,128)(2,1)}, u32[]{:S(2)}) %copy-start.6) | copy-done | bytes 65560
  5.7 0.8 %pack.1 = bf16[128,4,896]{2,1,0:T(4,128)(2,1)S(1)} custom-call(s32[1,128]{1,0:T(1,128)S(1)} %copy-done.8, s32[1,256]{1,0:T(1,128)S(1)} %bitcast.9, s32[256,128]{1,0:T(8,128)S(1)} %bitcast.8, s32[256,128]{1,0:T(8,128)S(1)} %copy-done.3, bf16[256,128]{1,0:T(8,128)(2,1)S(1)} %copy-done.5, bf16[256,128]{1,0:T(8,128)(2,1)S(1)} %copy-done.6, ...), custom_call_target="tpu_custom_call" | custom-call | tf_op jit(solution)/shard_map/pack/pallas_call | solution.py:41
  6.5 43.2 %all_to_all.16.in_ref = bf16[128,4,896]{2,1,0:T(4,128)(2,1)S(1)} all-to-all(bf16[128,4,896]{2,1,0:T(4,128)(2,1)S(1)} %pack.1), channel_id=1, replica_groups=mesh['owner'=128,'rep'=4] {'owner'}, dimensions={0} | all-to-all | bytes 1835008 | tf_op jit(solution)/shard_map/all_to_all | solution.py:147
  49.7 0.9 %route.1 = bf16[512,896]{1,0:T(8,128)(2,1)S(1)} custom-call(bf16[128,4,896]{2,1,0:T(4,128)(2,1)S(1)} %all_to_all.16.in_ref), custom_call_target="tpu_custom_call" | custom-call | tf_op jit(solution)/shard_map/route/pallas_call | solution.py:77
  50.6 0.0 copy-start
  50.6 0.0 copy-start.4
  50.6 19.1 %all_to_all.17 = bf16[4,128,896]{2,1,0:T(8,128)(2,1)S(1)} all-to-all(bf16[4,128,896]{2,1,0:T(8,128)(2,1)S(1)} %bitcast.5), channel_id=1, replica_groups=mesh['owner'=128,'rep'=4] {'rep'}, dimensions={0} | all-to-all | bytes 1835008 | tf_op jit(solution)/shard_map/all_to_all | solution.py:149
  69.7 0.0 copy-done
  69.7 0.0 copy-done.4
  69.7 8.9 %join.1 = (f32[64,4,512]{2,1,0:T(4,128)}, f32[64,512]{1,0:T(8,128)}) custom-call(bf16[512,896]{1,0:T(8,128)(2,1)S(1)} %bitcast.6, f32[64,4,512]{2,1,0:T(4,128)S(1)} %copy-done, f32[64,512]{1,0:T(8,128)S(1)} %copy-done.4), custom_call_target="tpu_custom_call" | custom-call | tf_op jit(solution)/shard_map/join/pallas_call | solution.py:139
Async XLA Ops:
  0.6 0.7 copy-start.7
  0.6 0.7 copy-start.8
  1.3 0.9 %copy-start.1 = (bf16[256,3,128]{2,0,1:T(8,128)(2,1)S(1)}, bf16[256,3,128]{2,0,1:T(8,128)(2,1)}, u32[]{:S(2)}) copy-start(bf16[256,3,128]{2,0,1:T(8,128)(2,1)} %param.14) | copy-start | bytes 589828
  2.2 0.9 %copy-start.2 = (s32[32768]{0:T(1024)S(1)}, s32[32768]{0:T(1024)}, u32[]{:S(2)}) copy-start(s32[32768]{0:T(1024)} %param.15) | copy-start | bytes 393220
  3.1 0.9 %copy-start.3 = (s32[256,128]{1,0:T(8,128)S(1)}, s32[256,128]{1,0:T(8,128)}, u32[]{:S(2)}) copy-start(s32[256,128]{1,0:T(8,128)} %voxel_ref.1) | copy-start | bytes 393220
  4.1 0.8 %copy-start.5 = (bf16[256,128]{1,0:T(8,128)(2,1)S(1)}, bf16[256,128]{1,0:T(8,128)(2,1)}, u32[]{:S(2)}) copy-start(bf16[256,128]{1,0:T(8,128)(2,1)} %sdf_ref.1) | copy-start | bytes 196612
  4.9 0.8 %copy-start.6 = (bf16[256,128]{1,0:T(8,128)(2,1)S(1)}, bf16[256,128]{1,0:T(8,128)(2,1)}, u32[]{:S(2)}) copy-start(bf16[256,128]{1,0:T(8,128)(2,1)} %weight_ref.2) | copy-start | bytes 196612
  50.6 19.1 %copy-start = (f32[64,4,512]{2,1,0:T(4,128)S(1)}, f32[64,4,512]{2,1,0:T(4,128)}, u32[]{:S(2)}) copy-start(f32[64,4,512]{2,1,0:T(4,128)} %tsdf_ref.1) | copy-start | bytes 1572868
  50.6 19.1 %copy-start.4 = (f32[64,512]{1,0:T(8,128)S(1)}, f32[64,512]{1,0:T(8,128)}, u32[]{:S(2)}) copy-start(f32[64,512]{1,0:T(8,128)} %weight_ref.3) | copy-start | bytes 393220

commit v2 on v0

v2 whole, which is shorter than its diff:
```python
import functools

import jax
import jax.numpy as jnp
from jax import lax
from jax.experimental import pallas as pl
from jax.experimental.pallas import tpu as pltpu
from jax.sharding import PartitionSpec as P

bf16 = jnp.bfloat16
f32 = jnp.float32
i32 = jnp.int32
OWN = 256
LANES = 128
UNIT = 8
WIDE = 8
PARAMS = pltpu.CompilerParams(vmem_limit_bytes=48 << 20)


def ids(shape, dim):
    return lax.broadcasted_iota(i32, shape, dim)


def dot(a, b, dims=((1,), (0,))):
    return lax.dot_general(a, b, (dims, ((), ())), preferred_element_type=f32)


def pack_kernel(*refs):
    sources, out_ref, held, sems = refs[:7], refs[7], refs[8:15], refs[15]
    copies = [
        pltpu.make_async_copy(a, b, sems.at[n]) for n, (a, b) in enumerate(zip(sources, held))
    ]
    for copy in copies:
        copy.start()
    counts_ref, blocks_ref, table_ref, voxel_ref, weight_ref, sdf_ref, color_ref = held
    owners = counts_ref.shape[1]
    bins = blocks_ref.shape[1]
    copies[0].wait()
    counts = jnp.broadcast_to(counts_ref[...], (owners, owners)).astype(f32)
    row, lane = ids((owners, owners), 0), ids((owners, owners), 1)
    ends = jnp.sum(jnp.where(lane <= row, counts, 0.0), axis=1, keepdims=True)
    own = jnp.sum(jnp.where(lane == row, counts, 0.0), axis=1, keepdims=True)
    bin_ids = ids((owners, bins), 1).astype(f32)
    passed = bin_ids >= ends
    target = jnp.sum(jnp.where(passed, 1.0, 0.0), axis=0, keepdims=True)
    before = jnp.sum(jnp.where(passed, own, 0.0), axis=0, keepdims=True)
    slot = (8.0 * target + bin_ids[:1] - before).astype(i32)
    select = jnp.where(ids((8 * owners, bins), 0) == slot, 1.0, 0.0).astype(bf16)
    copies[1].wait()
    copies[2].wait()
    blocks = blocks_ref[...]
    pick = jnp.where(ids((table_ref.shape[0], bins), 0) == blocks // LANES, 1.0, 0.0).astype(bf16)
    table = (table_ref[...] % OWN).astype(f32).astype(bf16)
    found = dot(table, pick, ((0,), (0,)))
    code = 1.0 + jnp.sum(
        jnp.where(ids((LANES, bins), 0) == blocks % LANES, found, 0.0), axis=0, keepdims=True
    )

    def put(channel, values):
        cut = values.reshape(owners, 8, LANES)[:, :4].astype(bf16)
        out_ref[:, :, channel * LANES : (channel + 1) * LANES] = cut

    put(6, dot(select, jnp.broadcast_to(code, (LANES, bins)).astype(bf16), ((1,), (1,))))
    for copy in copies[3:]:
        copy.wait()
    weight = weight_ref[...].astype(f32)
    features = [(voxel_ref[...] - 256).astype(f32).astype(bf16), weight_ref[...]]
    features.append((weight * sdf_ref[...].astype(f32)).astype(bf16))
    features += [(weight * color_ref[c].astype(f32)).astype(bf16) for c in range(3)]
    for c in range(0, 6, 2):
        pair = dot(select, jnp.concatenate(features[c : c + 2], axis=1))
        put(c, pair[:, :LANES])
        put(c + 1, pair[:, LANES:])


def pack(counts, blocks, table, voxel, weight, sdf, color):
    arrays = (
        counts,
        blocks.reshape(1, -1),
        table.reshape(-1, LANES),
        voxel,
        weight,
        sdf,
        color.transpose(1, 0, 2),
    )
    return pl.pallas_call(
        pack_kernel,
        out_shape=jax.ShapeDtypeStruct((counts.shape[1], 4, 7 * LANES), bf16),
        in_specs=[pl.BlockSpec(memory_space=pltpu.HBM)] * len(arrays),
        scratch_shapes=[pltpu.VMEM(a.shape, a.dtype) for a in arrays]
        + [pltpu.SemaphoreType.DMA((len(arrays),))],
        compiler_params=PARAMS,
        name="pack",
    )(*(pltpu.with_memory_space_constraint(a, pltpu.HBM) for a in arrays))


def rows_of(ref, channel):
    part = ref[:, :, channel * LANES : (channel + 1) * LANES]
    return part.reshape(4 * part.shape[0], LANES)


def route_kernel(in_ref, out_ref):
    replicas, height = out_ref.shape[:2]
    quota = height - 8
    share = OWN // replicas
    codes = rows_of(in_ref, 6)
    count = codes.shape[0]
    eye = jnp.where(ids((LANES, LANES), 0) == ids((LANES, LANES), 1), 1.0, 0.0)
    earlier = jnp.where(ids((LANES, LANES), 0) < ids((LANES, LANES), 1), 1.0, 0.0).astype(bf16)
    quarters = ids((8, LANES), 0).astype(f32)
    total = jnp.zeros((8, 1), f32)
    destinations, spots = [], []
    for g in range(count // LANES):
        block = codes[g * LANES : (g + 1) * LANES].astype(f32)
        code = jnp.sum(block * eye, axis=0, keepdims=True)
        live = code > 0.5
        quarter = jnp.where(live, jnp.floor((code - 1.0) * (1.0 / share)), 9.0)
        member = jnp.where(quarters == quarter, 1.0, 0.0)
        ahead = dot(member.astype(bf16), earlier) + total
        total = total + jnp.sum(member, axis=1, keepdims=True)
        rank = jnp.sum(ahead * member, axis=0, keepdims=True)
        destinations.append(jnp.where(live, quarter * quota + rank, -1.0))
        spots.append(jnp.where(live, code - quarter * share, 0.0))
    destination = jnp.concatenate(destinations, axis=1).astype(i32)
    spot = jnp.concatenate(spots, axis=1)
    select = jnp.where(ids((replicas * quota, count), 0) == destination, 1.0, 0.0).astype(bf16)
    placed = dot(jnp.broadcast_to(spot, (8, count)).astype(bf16), select, ((1,), (1,)))
    for q in range(replicas):
        out_ref[q, quota:, :LANES] = placed[:, q * quota : (q + 1) * quota].astype(bf16)
        out_ref[q, quota:, LANES:] = jnp.zeros((8, out_ref.shape[2] - LANES), bf16)
    for c in range(0, 6, 2):
        pair = jnp.concatenate([rows_of(in_ref, c), rows_of(in_ref, c + 1)], axis=1)
        moved = dot(select, pair).astype(bf16)
        for q in range(replicas):
            out_ref[q, :quota, c * LANES : (c + 2) * LANES] = moved[q * quota : (q + 1) * quota]


def route(arrived, replicas):
    quota = 4 * arrived.shape[0] // replicas
    return pl.pallas_call(
        route_kernel,
        out_shape=jax.ShapeDtypeStruct((replicas, quota + 8, 6 * LANES), bf16),
        compiler_params=PARAMS,
        name="route",
    )(arrived)


def join_kernel(
    in_ref, tsdf_ref, weight_ref, new_tsdf_hbm, new_weight_hbm,
    sums_ref, new_tsdf_ref, new_weight_ref, plan_ref, plan, sem, sems,
):
    places = weight_ref.shape[0]
    height = 136
    quota = height - 8
    groups = in_ref.shape[0] // height
    units = groups * quota // UNIT
    unit_row, unit_lane = ids((LANES, LANES), 0), ids((LANES, LANES), 1)
    live_units = jnp.zeros((LANES, LANES), f32)
    for r in range(groups):
        code = in_ref[r * height + quota : r * height + height, :LANES].astype(f32)[:1]
        live = jnp.where(code > 0.5, 1.0, 0.0)
        plan_ref[r : r + 1, :] = jnp.where(code > 0.5, code - 1.0, float(places)).astype(i32)
        bins = jnp.sum(live, axis=1, keepdims=True)
        first = ((unit_row - r * (quota // UNIT)) * UNIT).astype(f32)
        here = (unit_row >= r * (quota // UNIT)) & (unit_row < (r + 1) * (quota // UNIT))
        live_units = jnp.where(here & (first < bins), 1.0, live_units)
    plan_ref[groups : groups + 1, :] = jnp.full((1, LANES), places, i32)
    below = jnp.where(unit_lane < unit_row, 1.0, 0.0).astype(bf16)
    rank = dot(below, live_units.astype(bf16))
    chosen = (live_units > 0.5) & (rank == unit_lane.astype(f32))
    listed = jnp.sum(jnp.where(chosen, unit_row.astype(f32) + 1.0, 0.0), axis=0, keepdims=True)
    listed = jnp.where(listed > 0.5, listed - 1.0, float(units))
    plan_ref[groups + 1 : groups + 2, :] = listed.astype(i32)
    number = jnp.sum(live_units, axis=0, keepdims=True)
    plan_ref[groups + 2 : groups + 3, :] = number.astype(i32)
    copy = pltpu.make_async_copy(plan_ref, plan, sem)
    copy.start()
    sums_ref[...] = jnp.zeros_like(sums_ref)
    copy.wait()

    lanes = ids((LANES, LANES), 0).astype(f32).astype(bf16)
    sub = ids((8, LANES), 0)
    one, zero = jnp.ones((), bf16), jnp.zeros((), bf16)

    def halves(tiles, upper, lower, b):
        hot = jnp.where(lanes == jnp.broadcast_to(lower[b : b + 1], (LANES, LANES)), one, zero)
        feature = jnp.zeros((8, LANES), f32)
        for c in range(5):
            value = jnp.broadcast_to(tiles[1 + c][b : b + 1], (8, LANES))
            feature = jnp.where(sub == c, value, feature)
        level = jnp.broadcast_to(upper[b : b + 1], (8, LANES))
        left = [jnp.where(level == a, feature, 0.0) for a in range(4)]
        return hot, jnp.concatenate(left, axis=0).astype(bf16)

    def step(n, carry):
        for u in range(WIDE):
            unit = plan[groups + 1, n * WIDE + u]
            group = unit // (quota // UNIT)
            within = (unit % (quota // UNIT)) * UNIT
            start = jnp.where(unit < units, group * height + within, 0)
            start = pl.multiple_of(start, UNIT)
            tiles = [
                in_ref[pl.ds(start, UNIT), c * LANES : (c + 1) * LANES].astype(f32)
                for c in range(6)
            ]
            voxel = tiles[0] + 256.0
            upper = jnp.floor(voxel * (1.0 / LANES))
            lower = (voxel - upper * float(LANES)).astype(bf16)
            for b in range(0, UNIT, 2):
                hot_a, left_a = halves(tiles, upper, lower, b)
                hot_b, left_b = halves(tiles, upper, lower, b + 1)
                empty = jnp.zeros_like(left_a)
                left = jnp.concatenate(
                    [
                        jnp.concatenate([left_a, empty], axis=1),
                        jnp.concatenate([empty, left_b], axis=1),
                    ],
                    axis=0,
                )
                grids = dot(left, jnp.concatenate([hot_a, hot_b], axis=1), ((1,), (1,)))
                for k in range(2):
                    at = pl.multiple_of(plan[group, within + b + k] * 32, 32)
                    sums_ref[pl.ds(at, 32), :] += grids[k * 32 : (k + 1) * 32]
        return carry

    lax.fori_loop(0, (plan[groups + 2, 0] + WIDE - 1) // WIDE, step, 0)

    copies = []
    for a in range(4):
        cols = slice(a * LANES, (a + 1) * LANES)
        old = weight_ref[:, cols]
        new = old + sums_ref[pl.ds(a * 8, places, stride=32), :]
        new_weight_ref[:, cols] = new
        for c in range(4):
            share = sums_ref[pl.ds(a * 8 + 1 + c, places, stride=32), :]
            new_tsdf_ref[:, c, cols] = (old * tsdf_ref[:, c, cols] + share) / new
        copies.append(
            pltpu.make_async_copy(new_tsdf_ref.at[:, :, cols], new_tsdf_hbm.at[:, :, cols], sems.at[a])
        )
        copies[-1].start()
    copies.append(pltpu.make_async_copy(new_weight_ref, new_weight_hbm, sems.at[4]))
    copies[-1].start()
    for copy in copies:
        copy.wait()


def join(final, old_tsdf, old_weight):
    places = old_weight.shape[0]
    return pl.pallas_call(
        join_kernel,
        out_shape=(
            jax.ShapeDtypeStruct(old_tsdf.shape, f32),
            jax.ShapeDtypeStruct(old_weight.shape, f32),
        ),
        out_specs=(pl.BlockSpec(memory_space=pl.ANY), pl.BlockSpec(memory_space=pl.ANY)),
        scratch_shapes=[
            pltpu.VMEM(((places + 1) * 32, LANES), f32),
            pltpu.VMEM(old_tsdf.shape, f32),
            pltpu.VMEM(old_weight.shape, f32),
            pltpu.VMEM((8, LANES), i32),
            pltpu.SMEM((8, LANES), i32),
            pltpu.SemaphoreType.DMA(()),
            pltpu.SemaphoreType.DMA((5,)),
        ],
        compiler_params=PARAMS,
        name="join",
    )(final, old_tsdf, old_weight)


def local(
    bin_blocks, send_counts, voxel_index, point_sdf, point_weight, point_color, owner_table,
    old_tsdf, old_weight,
):
    packed = pack(
        send_counts, bin_blocks, owner_table, voxel_index, point_weight, point_sdf, point_color
    )
    arrived = lax.all_to_all(packed, "owner", split_axis=0, concat_axis=0, tiled=True)
    sent = route(arrived, lax.axis_size("rep"))
    final = lax.all_to_all(sent, "rep", split_axis=0, concat_axis=0, tiled=True)
    return join(final.reshape(-1, final.shape[2]), old_tsdf, old_weight)


def solution(mesh):
    both = ("owner", "rep")
    placed = (
        P(both),
        P(both, None),
        P(both, None),
        P(both, None),
        P(both, None),
        P(both, None, None),
        P(),
        P(both, None, None),
        P(both, None),
    )
    return jax.shard_map(
        local,
        mesh=mesh,
        in_specs=placed,
        out_specs=(P(both, None, None), P(both, None)),
        check_vma=False,
    )
```

time: 213 us -> 72.5 us (0.34)
  local copies, waits for them, and re-layouts: 69.7 us -> 0.01 us
  blocking collectives: 0 us -> 60.7 us
  waiting for transfers between devices: 45.5 us -> 0 us
  other arithmetic: 43.3 us -> 0 us
  starting transfers between devices: 39.6 us -> 0 us
  matrix products: 11 us -> 0 us
  Pallas kernels: 0 us -> 10.2 us
    all_to_all x0 -> x2, blocking collectives: none -> 60.7 us  [the longest x1 46.3 us: local(): lax.all_to_all(packed, 'owner', split_axis=0, concat_axis=0, tiled=True)]
    all_to_all x5 -> x0, waiting for transfers between devices: 45.5 us -> none  [the longest x2 29.5 us: in_one_piece(): lax.all_to_all(both, axis, split_axis=split_dim, concat_axis=concat_dim,...]
    all_to_all x5 -> x0, starting transfers between devices: 39.6 us -> none  [the longest x1 17.8 us: in_one_piece_2(): lax.all_to_all(both, axis, split_axis=split_dim, concat_axis=concat_dim,...]
    gather x14 -> x0, local copies, waits for them, and re-layouts: 29.4 us -> none  [the longest x3 6.75 us: local(): blocks_sent = jnp.where(active, owner_table[bin_blocks[source]] % OWN, -1)]
    scatter-add x4 -> x0, other arithmetic: 23.3 us -> none  [fold_group(): return (running.at[block_ids].add(slot_grids), None)]
    dot_general x4 -> x0, local copies, waits for them, and re-layouts: 12.6 us -> none  [fold_group(): jnp.einsum('gkp,gpb->gkb', left_side, right_side, preferred_element_type=...]
    select_n x22 -> x0, other arithmetic: 11.4 us -> none  [the longest x4 3.6 us: fold_group(): upper_part = voxel_rows // VB]
    dot_general x4 -> x0, matrix products: 11 us -> none  [fold_group(): jnp.einsum('gkp,gpb->gkb', left_side, right_side, preferred_element_type=...]
  transfers between devices with their start and end apart: 5 -> 0, of which waited for: 4 -> 0; matrix products, arithmetic and copies ran while one was open for 15% -> 0% of each run, Pallas kernels for 0% -> 0%
where the time goes in v2:
time: 72.5 us; the launch traced here: 71.6 us
  blocking collectives  60.7 us (84%)
  Pallas kernels  10.2 us (14%)
    all_to_all x1, blocking collectives, local(): lax.all_to_all(packed, 'owner', split_axis=0, concat_axis=0, tiled=True)  46.3 us
    all_to_all x1, blocking collectives, local(): final = lax.all_to_all(sent, 'rep', split_axis=0, concat_axis=0, tiled=True)  14.4 us
    pallas_call x1, Pallas kernels, join(): pl.pallas_call(join_kernel, out_shape=(jax.ShapeDtypeStruct(old_tsdf.shap...  6.92 us
    pallas_call x1, Pallas kernels, pack(): pl.pallas_call(pack_kernel, out_shape=jax.ShapeDtypeStruct((counts.shape[...  2.36 us

profile of v2, /device:TPU:6, one launch (start us, length us, event | category | flops | bytes accessed | tf_op | source)
XLA Modules:
  0.0 71.6 jit_solution(17977014729370614521)
XLA Ops:
  0.6 2.4 %pack.1 = bf16[128,4,896]{2,1,0:T(4,128)(2,1)S(1)} custom-call(s32[1,128]{1,0:T(1,128)} %refs_0_.1, s32[1,256]{1,0:T(1,128)} %bitcast.7, s32[256,128]{1,0:T(8,128)} %bitcast.6, s32[256,128]{1,0:T(8,128)} %refs_3_.1, bf16[256,128]{1,0:T(8,128)(2,1)} %refs_4_.1, bf16[256,128]{1,0:T(8,128)(2,1)} %refs_5_.1, bf16[3,256,128]{2,1,0:T(8,128)(2,1)} %bitcast.5), custom_call_target="tpu_custom_call" | custom-call | tf_op jit(solution)/shard_map/pack/pallas_call | solution.py:86
  3.0 46.3 %all_to_all.10.in_ref = bf16[128,4,896]{2,1,0:T(4,128)(2,1)S(1)} all-to-all(bf16[128,4,896]{2,1,0:T(4,128)(2,1)S(1)} %pack.1), channel_id=1, replica_groups=mesh['owner'=128,'rep'=4] {'owner'}, dimensions={0} | all-to-all | bytes 1835008 | tf_op jit(solution)/shard_map/all_to_all | solution.py:277
  49.3 0.9 %route.1 = bf16[4,136,768]{2,1,0:T(8,128)(2,1)S(1)} custom-call(bf16[128,4,896]{2,1,0:T(4,128)(2,1)S(1)} %all_to_all.10.in_ref), custom_call_target="tpu_custom_call" | custom-call | tf_op jit(solution)/shard_map/route/pallas_call | solution.py:140
  50.2 0.0 copy-start
  50.2 0.0 copy-start.1
  50.3 14.4 %all_to_all.11 = bf16[4,136,768]{2,1,0:T(8,128)(2,1)S(1)} all-to-all(bf16[4,136,768]{2,1,0:T(8,128)(2,1)S(1)} %route.1), channel_id=1, replica_groups=mesh['owner'=128,'rep'=4] {'rep'}, dimensions={0} | all-to-all | bytes 1671168 | tf_op jit(solution)/shard_map/all_to_all | solution.py:279
  64.6 0.0 copy-done
  64.6 0.0 copy-done.1
  64.6 6.9 %join.1 = (f32[64,4,512]{2,1,0:T(4,128)}, f32[64,512]{1,0:T(8,128)}) custom-call(bf16[544,768]{1,0:T(8,128)(2,1)S(1)} %bitcast.4, f32[64,4,512]{2,1,0:T(4,128)S(1)} %copy-done, f32[64,512]{1,0:T(8,128)S(1)} %copy-done.1), custom_call_target="tpu_custom_call" | custom-call | tf_op jit(solution)/shard_map/join/pallas_call | solution.py:249
Async XLA Ops:
  50.2 14.4 %copy-start = (f32[64,4,512]{2,1,0:T(4,128)S(1)}, f32[64,4,512]{2,1,0:T(4,128)}, u32[]{:S(2)}) copy-start(f32[64,4,512]{2,1,0:T(4,128)} %tsdf_ref.1) | copy-start | bytes 1572868
  50.2 14.4 %copy-start.1 = (f32[64,512]{1,0:T(8,128)S(1)}, f32[64,512]{1,0:T(8,128)}, u32[]{:S(2)}) copy-start(f32[64,512]{1,0:T(8,128)} %weight_ref.1) | copy-start | bytes 393220

commit v3 on v2

--- a/solution.py
+++ b/solution.py
@@ -57,10 +57,15 @@
     )
 
     def put(channel, values):
-        cut = values.reshape(owners, 8, LANES)[:, :4].astype(bf16)
-        out_ref[:, :, channel * LANES : (channel + 1) * LANES] = cut
-
-    put(6, dot(select, jnp.broadcast_to(code, (LANES, bins)).astype(bf16), ((1,), (1,))))
+        rows = values.reshape(owners, 8, LANES)
+        for h in range(2):
+            at = (h * 6 + channel) * LANES
+            out_ref[:, :, at : at + LANES] = rows[:, 2 * h : 2 * h + 2].astype(bf16)
+
+    coded = dot(select, jnp.broadcast_to(code, (LANES, bins)).astype(bf16), ((1,), (1,)))
+    coded = coded.reshape(owners, 8, LANES)
+    first = ids((owners, 2, LANES), 2) == 0
+    out_ref[:, :, 12 * LANES :] = jnp.where(first, coded[:, :2], coded[:, 2:4]).astype(bf16)
     for copy in copies[3:]:
         copy.wait()
     weight = weight_ref[...].astype(f32)
@@ -85,7 +90,7 @@
     )
     return pl.pallas_call(
         pack_kernel,
-        out_shape=jax.ShapeDtypeStruct((counts.shape[1], 4, 7 * LANES), bf16),
+        out_shape=jax.ShapeDtypeStruct((counts.shape[1], 2, 13 * LANES), bf16),
         in_specs=[pl.BlockSpec(memory_space=pltpu.HBM)] * len(arrays),
         scratch_shapes=[pltpu.VMEM(a.shape, a.dtype) for a in arrays]
         + [pltpu.SemaphoreType.DMA((len(arrays),))],
@@ -94,25 +99,34 @@
     )(*(pltpu.with_memory_space_constraint(a, pltpu.HBM) for a in arrays))
 
 
-def rows_of(ref, channel):
-    part = ref[:, :, channel * LANES : (channel + 1) * LANES]
-    return part.reshape(4 * part.shape[0], LANES)
+def rows_of(ref, tile):
+    part = ref[:, :, tile * LANES : (tile + 1) * LANES]
+    return part.reshape(2 * part.shape[0], LANES)
+
+
+def both_rows(ref, channel):
+    return jnp.concatenate([rows_of(ref, channel), rows_of(ref, 6 + channel)], axis=0)
 
 
 def route_kernel(in_ref, out_ref):
     replicas, height = out_ref.shape[:2]
     quota = height - 8
     share = OWN // replicas
-    codes = rows_of(in_ref, 6)
-    count = codes.shape[0]
-    eye = jnp.where(ids((LANES, LANES), 0) == ids((LANES, LANES), 1), 1.0, 0.0)
+    tile = rows_of(in_ref, 12)
+    count = 2 * tile.shape[0]
+    codes = jnp.concatenate(
+        [
+            dot(jnp.where(ids((8, LANES), 1) == h, 1.0, 0.0).astype(bf16), tile, ((1,), (1,)))[:1]
+            for h in range(2)
+        ],
+        axis=1,
+    )
     earlier = jnp.where(ids((LANES, LANES), 0) < ids((LANES, LANES), 1), 1.0, 0.0).astype(bf16)
     quarters = ids((8, LANES), 0).astype(f32)
     total = jnp.zeros((8, 1), f32)
     destinations, spots = [], []
     for g in range(count // LANES):
-        block = codes[g * LANES : (g + 1) * LANES].astype(f32)
-        code = jnp.sum(block * eye, axis=0, keepdims=True)
+        code = codes[:, g * LANES : (g + 1) * LANES]
         live = code > 0.5
         quarter = jnp.where(live, jnp.floor((code - 1.0) * (1.0 / share)), 9.0)
         member = jnp.where(quarters == quarter, 1.0, 0.0)
@@ -129,7 +143,7 @@
         out_ref[q, quota:, :LANES] = placed[:, q * quota : (q + 1) * quota].astype(bf16)
         out_ref[q, quota:, LANES:] = jnp.zeros((8, out_ref.shape[2] - LANES), bf16)
     for c in range(0, 6, 2):
-        pair = jnp.concatenate([rows_of(in_ref, c), rows_of(in_ref, c + 1)], axis=1)
+        pair = jnp.concatenate([both_rows(in_ref, c), both_rows(in_ref, c + 1)], axis=1)
         moved = dot(select, pair).astype(bf16)
         for q in range(replicas):
             out_ref[q, :quota, c * LANES : (c + 2) * LANES] = moved[q * quota : (q + 1) * quota]

time: 72.5 us -> 71.4 us (0.985)
  blocking collectives: 60.7 us -> 59.4 us
    all_to_all x1, blocking collectives: 46.3 us -> 44.9 us  [local(): lax.all_to_all(packed, 'owner', split_axis=0, concat_axis=0, tiled=True)]
where the time goes in v3:
time: 71.4 us; the launch traced here: 70.4 us
  blocking collectives  59.4 us (83%)
  Pallas kernels  10.4 us (15%)
    all_to_all x1, blocking collectives, local(): lax.all_to_all(packed, 'owner', split_axis=0, concat_axis=0, tiled=True)  44.9 us
    all_to_all x1, blocking collectives, local(): final = lax.all_to_all(sent, 'rep', split_axis=0, concat_axis=0, tiled=True)  14.4 us
    pallas_call x1, Pallas kernels, join(): pl.pallas_call(join_kernel, out_shape=(jax.ShapeDtypeStruct(old_tsdf.shap...  6.92 us
    pallas_call x1, Pallas kernels, pack(): pl.pallas_call(pack_kernel, out_shape=jax.ShapeDtypeStruct((counts.shape[...  2.4 us

profile of v3, /device:TPU:6, one launch (start us, length us, event | category | flops | bytes accessed | tf_op | source)
XLA Modules:
  0.0 70.4 jit_solution(1910588525576491325)
XLA Ops:
  0.6 2.4 %pack.1 = bf16[128,2,1664]{2,1,0:T(2,128)(2,1)S(1)} custom-call(s32[1,128]{1,0:T(1,128)} %refs_0_.1, s32[1,256]{1,0:T(1,128)} %bitcast.7, s32[256,128]{1,0:T(8,128)} %bitcast.6, s32[256,128]{1,0:T(8,128)} %refs_3_.1, bf16[256,128]{1,0:T(8,128)(2,1)} %refs_4_.1, bf16[256,128]{1,0:T(8,128)(2,1)} %refs_5_.1, bf16[3,256,128]{2,1,0:T(8,128)(2,1)} %bitcast.5), custom_call_target="tpu_custom_call" | custom-call | tf_op jit(solution)/shard_map/pack/pallas_call | solution.py:91
  3.0 44.9 %all_to_all.10.in_ref = bf16[128,2,1664]{2,1,0:T(2,128)(2,1)S(1)} all-to-all(bf16[128,2,1664]{2,1,0:T(2,128)(2,1)S(1)} %pack.1), channel_id=1, replica_groups=mesh['owner'=128,'rep'=4] {'owner'}, dimensions={0} | all-to-all | bytes 1703936 | tf_op jit(solution)/shard_map/all_to_all | solution.py:291
  48.0 1.1 %route.1 = bf16[4,136,768]{2,1,0:T(8,128)(2,1)S(1)} custom-call(bf16[128,2,1664]{2,1,0:T(2,128)(2,1)S(1)} %all_to_all.10.in_ref), custom_call_target="tpu_custom_call" | custom-call | tf_op jit(solution)/shard_map/route/pallas_call | solution.py:154
  49.1 0.0 copy-start
  49.1 0.0 copy-start.1
  49.1 14.4 %all_to_all.11 = bf16[4,136,768]{2,1,0:T(8,128)(2,1)S(1)} all-to-all(bf16[4,136,768]{2,1,0:T(8,128)(2,1)S(1)} %route.1), channel_id=1, replica_groups=mesh['owner'=128,'rep'=4] {'rep'}, dimensions={0} | all-to-all | bytes 1671168 | tf_op jit(solution)/shard_map/all_to_all | solution.py:293
  63.5 0.0 copy-done
  63.5 0.0 copy-done.1
  63.5 6.9 %join.1 = (f32[64,4,512]{2,1,0:T(4,128)}, f32[64,512]{1,0:T(8,128)}) custom-call(bf16[544,768]{1,0:T(8,128)(2,1)S(1)} %bitcast.4, f32[64,4,512]{2,1,0:T(4,128)S(1)} %copy-done, f32[64,512]{1,0:T(8,128)S(1)} %copy-done.1), custom_call_target="tpu_custom_call" | custom-call | tf_op jit(solution)/shard_map/join/pallas_call | solution.py:263
Async XLA Ops:
  49.1 14.4 %copy-start = (f32[64,4,512]{2,1,0:T(4,128)S(1)}, f32[64,4,512]{2,1,0:T(4,128)}, u32[]{:S(2)}) copy-start(f32[64,4,512]{2,1,0:T(4,128)} %tsdf_ref.1) | copy-start | bytes 1572868
  49.1 14.4 %copy-start.1 = (f32[64,512]{1,0:T(8,128)S(1)}, f32[64,512]{1,0:T(8,128)}, u32[]{:S(2)}) copy-start(f32[64,512]{1,0:T(8,128)} %weight_ref.1) | copy-start | bytes 393220

commit v4 on v3

--- a/solution.py
+++ b/solution.py
@@ -108,7 +108,7 @@
     return jnp.concatenate([rows_of(ref, channel), rows_of(ref, 6 + channel)], axis=0)
 
 
-def route_kernel(in_ref, out_ref):
+def route_kernel(in_ref, out_ref, mine_ref):
     replicas, height = out_ref.shape[:2]
     quota = height - 8
     share = OWN // replicas
@@ -147,38 +147,37 @@
         moved = dot(select, pair).astype(bf16)
         for q in range(replicas):
             out_ref[q, :quota, c * LANES : (c + 2) * LANES] = moved[q * quota : (q + 1) * quota]
+    mine_ref[0] = out_ref[lax.axis_index("rep")]
 
 
 def route(arrived, replicas):
     quota = 4 * arrived.shape[0] // replicas
     return pl.pallas_call(
         route_kernel,
-        out_shape=jax.ShapeDtypeStruct((replicas, quota + 8, 6 * LANES), bf16),
+        out_shape=[jax.ShapeDtypeStruct((n, quota + 8, 6 * LANES), bf16) for n in (replicas, 1)],
         compiler_params=PARAMS,
         name="route",
     )(arrived)
 
 
-def join_kernel(
-    in_ref, tsdf_ref, weight_ref, new_tsdf_hbm, new_weight_hbm,
-    sums_ref, new_tsdf_ref, new_weight_ref, plan_ref, plan, sem, sems,
-):
-    places = weight_ref.shape[0]
-    height = 136
+def add_bins(in_ref, sums_ref, plan_ref, plan, sem, skipped, meanwhile):
+    groups, height = in_ref.shape[:2]
     quota = height - 8
-    groups = in_ref.shape[0] // height
-    units = groups * quota // UNIT
+    spare = sums_ref.shape[0] // 32 - 1
+    each = quota // UNIT
+    units = groups * each
     unit_row, unit_lane = ids((LANES, LANES), 0), ids((LANES, LANES), 1)
     live_units = jnp.zeros((LANES, LANES), f32)
     for r in range(groups):
-        code = in_ref[r * height + quota : r * height + height, :LANES].astype(f32)[:1]
+        code = in_ref[r, quota:, :LANES].astype(f32)[:1]
         live = jnp.where(code > 0.5, 1.0, 0.0)
-        plan_ref[r : r + 1, :] = jnp.where(code > 0.5, code - 1.0, float(places)).astype(i32)
+        plan_ref[r : r + 1, :] = jnp.where(code > 0.5, code - 1.0, float(spare)).astype(i32)
         bins = jnp.sum(live, axis=1, keepdims=True)
-        first = ((unit_row - r * (quota // UNIT)) * UNIT).astype(f32)
-        here = (unit_row >= r * (quota // UNIT)) & (unit_row < (r + 1) * (quota // UNIT))
+        bins = bins * jnp.where(skipped == r, 0.0, 1.0)
+        first = ((unit_row - r * each) * UNIT).astype(f32)
+        here = (unit_row >= r * each) & (unit_row < (r + 1) * each)
         live_units = jnp.where(here & (first < bins), 1.0, live_units)
-    plan_ref[groups : groups + 1, :] = jnp.full((1, LANES), places, i32)
+    plan_ref[groups : groups + 1, :] = jnp.full((1, LANES), spare, i32)
     below = jnp.where(unit_lane < unit_row, 1.0, 0.0).astype(bf16)
     rank = dot(below, live_units.astype(bf16))
     chosen = (live_units > 0.5) & (rank == unit_lane.astype(f32))
@@ -189,7 +188,7 @@
     plan_ref[groups + 2 : groups + 3, :] = number.astype(i32)
     copy = pltpu.make_async_copy(plan_ref, plan, sem)
     copy.start()
-    sums_ref[...] = jnp.zeros_like(sums_ref)
+    meanwhile()
     copy.wait()
 
     lanes = ids((LANES, LANES), 0).astype(f32).astype(bf16)
@@ -209,13 +208,12 @@
     def step(n, carry):
         for u in range(WIDE):
             unit = plan[groups + 1, n * WIDE + u]
-            group = unit // (quota // UNIT)
-            within = (unit % (quota // UNIT)) * UNIT
-            start = jnp.where(unit < units, group * height + within, 0)
-            start = pl.multiple_of(start, UNIT)
+            group = unit // each
+            within = (unit % each) * UNIT
+            source = jnp.minimum(group, groups - 1)
+            rows = pl.ds(pl.multiple_of(within, UNIT), UNIT)
             tiles = [
-                in_ref[pl.ds(start, UNIT), c * LANES : (c + 1) * LANES].astype(f32)
-                for c in range(6)
+                in_ref[source, rows, c * LANES : (c + 1) * LANES].astype(f32) for c in range(6)
             ]
             voxel = tiles[0] + 256.0
             upper = jnp.floor(voxel * (1.0 / LANES))
@@ -239,17 +237,62 @@
 
     lax.fori_loop(0, (plan[groups + 2, 0] + WIDE - 1) // WIDE, step, 0)
 
+
+PLAN = [
+    pltpu.VMEM((8, LANES), i32),
+    pltpu.SMEM((8, LANES), i32),
+    pltpu.SemaphoreType.DMA(()),
+]
+
+
+def begin_kernel(in_ref, tsdf_ref, weight_ref, sums_ref, plan_ref, plan, sem):
+    places = weight_ref.shape[0]
+
+    def lay():
+        sums_ref[...] = jnp.zeros_like(sums_ref)
+        for a in range(4):
+            cols = slice(a * LANES, (a + 1) * LANES)
+            old = weight_ref[:, cols]
+            sums_ref[pl.ds(a * 8, places, stride=32), :] = old
+            for c in range(4):
+                at = pl.ds(a * 8 + 1 + c, places, stride=32)
+                sums_ref[at, :] = old * tsdf_ref[:, c, cols]
+
+    add_bins(in_ref, sums_ref, plan_ref, plan, sem, -1, lay)
+
+
+def begin(mine, old_tsdf, old_weight):
+    return pl.pallas_call(
+        begin_kernel,
+        out_shape=jax.ShapeDtypeStruct(((old_weight.shape[0] + 1) * 32, LANES), f32),
+        scratch_shapes=PLAN,
+        compiler_params=PARAMS,
+        name="begin",
+    )(mine, old_tsdf, old_weight)
+
+
+def join_kernel(
+    in_ref, begun_ref, new_tsdf_hbm, new_weight_hbm,
+    sums_ref, new_tsdf_ref, new_weight_ref, plan_ref, plan, sem, sems,
+):
+    places = new_weight_ref.shape[0]
+
+    def clear():
+        sums_ref[...] = jnp.zeros_like(sums_ref)
+
+    add_bins(in_ref, sums_ref, plan_ref, plan, sem, lax.axis_index("rep"), clear)
     copies = []
     for a in range(4):
         cols = slice(a * LANES, (a + 1) * LANES)
-        old = weight_ref[:, cols]
-        new = old + sums_ref[pl.ds(a * 8, places, stride=32), :]
+        at = [pl.ds(a * 8 + c, places, stride=32) for c in range(5)]
+        new = begun_ref[at[0], :] + sums_ref[at[0], :]
         new_weight_ref[:, cols] = new
         for c in range(4):
-            share = sums_ref[pl.ds(a * 8 + 1 + c, places, stride=32), :]
-            new_tsdf_ref[:, c, cols] = (old * tsdf_ref[:, c, cols] + share) / new
+            new_tsdf_ref[:, c, cols] = (begun_ref[at[1 + c], :] + sums_ref[at[1 + c], :]) / new
         copies.append(
-            pltpu.make_async_copy(new_tsdf_ref.at[:, :, cols], new_tsdf_hbm.at[:, :, cols], sems.at[a])
+            pltpu.make_async_copy(
+                new_tsdf_ref.at[:, :, cols], new_tsdf_hbm.at[:, :, cols], sems.at[a]
+            )
         )
         copies[-1].start()
     copies.append(pltpu.make_async_copy(new_weight_ref, new_weight_hbm, sems.at[4]))
@@ -258,27 +301,21 @@
         copy.wait()
 
 
-def join(final, old_tsdf, old_weight):
-    places = old_weight.shape[0]
+def join(final, begun, tsdf, weight):
     return pl.pallas_call(
         join_kernel,
-        out_shape=(
-            jax.ShapeDtypeStruct(old_tsdf.shape, f32),
-            jax.ShapeDtypeStruct(old_weight.shape, f32),
-        ),
+        out_shape=(tsdf, weight),
         out_specs=(pl.BlockSpec(memory_space=pl.ANY), pl.BlockSpec(memory_space=pl.ANY)),
         scratch_shapes=[
-            pltpu.VMEM(((places + 1) * 32, LANES), f32),
-            pltpu.VMEM(old_tsdf.shape, f32),
-            pltpu.VMEM(old_weight.shape, f32),
-            pltpu.VMEM((8, LANES), i32),
-            pltpu.SMEM((8, LANES), i32),
-            pltpu.SemaphoreType.DMA(()),
+            pltpu.VMEM(begun.shape, f32),
+            pltpu.VMEM(tsdf.shape, f32),
+            pltpu.VMEM(weight.shape, f32),
+            *PLAN,
             pltpu.SemaphoreType.DMA((5,)),
         ],
         compiler_params=PARAMS,
         name="join",
-    )(final, old_tsdf, old_weight)
+    )(final, begun)
 
 
 def local(
@@ -289,9 +326,11 @@
         send_counts, bin_blocks, owner_table, voxel_index, point_weight, point_sdf, point_color
     )
     arrived = lax.all_to_all(packed, "owner", split_axis=0, concat_axis=0, tiled=True)
-    sent = route(arrived, lax.axis_size("rep"))
+    sent, mine = route(arrived, lax.axis_size("rep"))
     final = lax.all_to_all(sent, "rep", split_axis=0, concat_axis=0, tiled=True)
-    return join(final.reshape(-1, final.shape[2]), old_tsdf, old_weight)
+    begun = begin(mine, old_tsdf, old_weight)
+    shapes = [jax.ShapeDtypeStruct(a.shape, a.dtype) for a in (old_tsdf, old_weight)]
+    return join(final, begun, *shapes)
 
 
 def solution(mesh):

time: 71.4 us -> 71.9 us (level)
  blocking collectives: 59.4 us -> 44.9 us
  waiting for transfers between devices: 0 us -> 7.78 us
  starting transfers between devices: 0 us -> 4.75 us
  Pallas kernels: 10.4 us -> 12.8 us
    all_to_all x1 -> x0, blocking collectives: 14.4 us -> none  [local(): final = lax.all_to_all(sent, 'rep', split_axis=0, concat_axis=0, tiled=True)]
    all_to_all x0 -> x1, waiting for transfers between devices: none -> 7.78 us  [local(): final = lax.all_to_all(sent, 'rep', split_axis=0, concat_axis=0, tiled=True)]
    all_to_all x0 -> x1, starting transfers between devices: none -> 4.75 us  [local(): final = lax.all_to_all(sent, 'rep', split_axis=0, concat_axis=0, tiled=True)]
    pallas_call x2 -> x3, Pallas kernels: 8 us -> 10.3 us  [the longest x1 6.38 us: join(): pl.pallas_call(join_kernel, out_shape=(tsdf, weight), out_specs=(pl.Block...]
  transfers between devices with their start and end apart: 0 -> 1, of which waited for: 0 -> 1; matrix products, arithmetic and copies ran while one was open for 0% -> 0% of each run, Pallas kernels for 0% -> 3%
where the time goes in v4:
time: 71.9 us; the launch traced here: 70.9 us
  blocking collectives  44.9 us (62%)
  Pallas kernels  12.8 us (18%)
  waiting for transfers between devices  7.78 us (11%)
  starting transfers between devices  4.75 us (7%)
    all_to_all x1, blocking collectives, local(): lax.all_to_all(packed, 'owner', split_axis=0, concat_axis=0, tiled=True)  44.9 us
    all_to_all x1, waiting for transfers between devices, local(): final = lax.all_to_all(sent, 'rep', split_axis=0, concat_axis=0, tiled=True)  7.78 us
    pallas_call x1, Pallas kernels, join(): pl.pallas_call(join_kernel, out_shape=(tsdf, weight), out_specs=(pl.Block...  6.38 us
    all_to_all x1, starting transfers between devices, local(): final = lax.all_to_all(sent, 'rep', split_axis=0, concat_axis=0, tiled=True)  4.75 us
    pallas_call x1, Pallas kernels, pack(): pl.pallas_call(pack_kernel, out_shape=jax.ShapeDtypeStruct((counts.shape[...  2.4 us
    pallas_call x1, Pallas kernels, route(): pl.pallas_call(route_kernel, out_shape=[jax.ShapeDtypeStruct((n, quota +...  2.05 us
    pallas_call x1, Pallas kernels, begin(): pl.pallas_call(begin_kernel, out_shape=jax.ShapeDtypeStruct(((old_weight....  1.92 us
  transfers between devices with their start and end apart: 1, of which 1 were waited for; matrix products, arithmetic and copies ran while one was open for 0% of the time, Pallas kernels for 3%

profile of v4, /device:TPU:6, one launch (start us, length us, event | category | flops | bytes accessed | tf_op | source)
XLA Modules:
  0.0 70.9 jit_solution(11468773940221912781)
XLA Ops:
  0.6 2.4 %pack.1 = bf16[128,2,1664]{2,1,0:T(2,128)(2,1)S(1)} custom-call(s32[1,128]{1,0:T(1,128)} %refs_0_.1, s32[1,256]{1,0:T(1,128)} %bitcast.5, s32[256,128]{1,0:T(8,128)} %bitcast.4, s32[256,128]{1,0:T(8,128)} %refs_3_.1, bf16[256,128]{1,0:T(8,128)(2,1)} %refs_4_.1, bf16[256,128]{1,0:T(8,128)(2,1)} %refs_5_.1, bf16[3,256,128]{2,1,0:T(8,128)(2,1)} %bitcast.3), custom_call_target="tpu_custom_call" | custom-call | tf_op jit(solution)/shard_map/pack/pallas_call | solution.py:91
  3.0 44.9 %all_to_all.10.in_ref = bf16[128,2,1664]{2,1,0:T(2,128)(2,1)S(1)} all-to-all(bf16[128,2,1664]{2,1,0:T(2,128)(2,1)S(1)} %pack.1), channel_id=1, replica_groups=mesh['owner'=128,'rep'=4] {'owner'}, dimensions={0} | all-to-all | bytes 1703936 | tf_op jit(solution)/shard_map/all_to_all | solution.py:328
  48.0 0.0 copy-start
  48.0 0.0 copy-start.1
  48.0 2.0 %route.1 = (bf16[4,136,768]{2,1,0:T(8,128)(2,1)}, bf16[1,136,768]{2,1,0:T(8,128)(2,1)S(1)}) custom-call(bf16[128,2,1664]{2,1,0:T(2,128)(2,1)S(1)} %all_to_all.10.in_ref), custom_call_target="tpu_custom_call" | custom-call | tf_op jit(solution)/shard_map/route/pallas_call | solution.py:155
  50.0 4.7 %all-to-all-start.1 = ((bf16[4,136,768]{2,1,0:T(8,128)(2,1)}), bf16[4,136,768]{2,1,0:T(8,128)(2,1)S(1)}, u32[]{:S(2)}, u32[]{:S(2)}) async-start(bf16[4,136,768]{2,1,0:T(8,128)(2,1)} %get-tuple-element.4), calls=%async_computation.1 | async-start | bytes 1671168 | tf_op jit(solution)/shard_map/all_to_all | solution.py:330
  54.8 0.0 copy-done
  54.8 0.0 copy-done.1
  54.8 1.9 %begin.1.begun_ref = f32[2080,128]{1,0:T(8,128)S(1)} custom-call(bf16[1,136,768]{2,1,0:T(8,128)(2,1)S(1)} %get-tuple-element.5.in_ref, f32[64,4,512]{2,1,0:T(4,128)S(1)} %copy-done, f32[64,512]{1,0:T(8,128)S(1)} %copy-done.1), custom_call_target="tpu_custom_call" | custom-call | tf_op jit(solution)/shard_map/begin/pallas_call | solution.py:265
  56.7 7.8 %all-to-all-done.1.in_ref = bf16[4,136,768]{2,1,0:T(8,128)(2,1)S(1)} async-done(((bf16[4,136,768]{2,1,0:T(8,128)(2,1)}), bf16[4,136,768]{2,1,0:T(8,128)(2,1)S(1)}, u32[]{:S(2)}, u32[]{:S(2)}) %all-to-all-start.1) | async-done | bytes 835616 | tf_op jit(solution)/shard_map/all_to_all | solution.py:330
  64.5 6.4 %join.1 = (f32[64,4,512]{2,1,0:T(4,128)}, f32[64,512]{1,0:T(8,128)}) custom-call(bf16[4,136,768]{2,1,0:T(8,128)(2,1)S(1)} %all-to-all-done.1.in_ref, f32[2080,128]{1,0:T(8,128)S(1)} %begin.1.begun_ref), custom_call_target="tpu_custom_call" | custom-call | tf_op jit(solution)/shard_map/join/pallas_call | solution.py:305
Async XLA Ops:
  48.0 6.8 %copy-start = (f32[64,4,512]{2,1,0:T(4,128)S(1)}, f32[64,4,512]{2,1,0:T(4,128)}, u32[]{:S(2)}) copy-start(f32[64,4,512]{2,1,0:T(4,128)} %tsdf_ref.1) | copy-start | bytes 1572868
  48.0 6.8 %copy-start.1 = (f32[64,512]{1,0:T(8,128)S(1)}, f32[64,512]{1,0:T(8,128)}, u32[]{:S(2)}) copy-start(f32[64,512]{1,0:T(8,128)} %weight_ref.1) | copy-start | bytes 393220
  50.0 14.5 %all-to-all-start.1 = ((bf16[4,136,768]{2,1,0:T(8,128)(2,1)}), bf16[4,136,768]{2,1,0:T(8,128)(2,1)S(1)}, u32[]{:S(2)}, u32[]{:S(2)}) async-start(bf16[4,136,768]{2,1,0:T(8,128)(2,1)} %get-tuple-element.4), calls=%async_computation.1 | async-start | bytes 1671168 | tf_op jit(solution)/shard_map/all_to_all | solution.py:330

commit v5 on v3

--- a/solution.py
+++ b/solution.py
@@ -14,6 +14,9 @@
 LANES = 128
 UNIT = 8
 WIDE = 8
+HALF = 64
+DEEP = 40
+PART = 16
 PARAMS = pltpu.CompilerParams(vmem_limit_bytes=48 << 20)
 
 
@@ -44,8 +47,10 @@
     passed = bin_ids >= ends
     target = jnp.sum(jnp.where(passed, 1.0, 0.0), axis=0, keepdims=True)
     before = jnp.sum(jnp.where(passed, own, 0.0), axis=0, keepdims=True)
-    slot = (8.0 * target + bin_ids[:1] - before).astype(i32)
-    select = jnp.where(ids((8 * owners, bins), 0) == slot, 1.0, 0.0).astype(bf16)
+    position = bin_ids[:1] - before
+    second = jnp.where(position > 1.5, 1.0, 0.0)
+    slot = (2.0 * target + position + second * (2.0 * owners - 2.0)).astype(i32)
+    select = jnp.where(ids((4 * owners, bins), 0) == slot, 1.0, 0.0).astype(bf16)
     copies[1].wait()
     copies[2].wait()
     blocks = blocks_ref[...]
@@ -56,16 +61,19 @@
         jnp.where(ids((LANES, bins), 0) == blocks % LANES, found, 0.0), axis=0, keepdims=True
     )
 
+    def cut(values, h):
+        half = values[h * 2 * owners : (h + 1) * 2 * owners]
+        return half.astype(bf16).reshape(owners, 2, LANES)
+
     def put(channel, values):
-        rows = values.reshape(owners, 8, LANES)
         for h in range(2):
             at = (h * 6 + channel) * LANES
-            out_ref[:, :, at : at + LANES] = rows[:, 2 * h : 2 * h + 2].astype(bf16)
+            out_ref[:, :, at : at + LANES] = cut(values, h)
 
     coded = dot(select, jnp.broadcast_to(code, (LANES, bins)).astype(bf16), ((1,), (1,)))
-    coded = coded.reshape(owners, 8, LANES)
-    first = ids((owners, 2, LANES), 2) == 0
-    out_ref[:, :, 12 * LANES :] = jnp.where(first, coded[:, :2], coded[:, 2:4]).astype(bf16)
+    first = ids((2 * owners, LANES), 1) == 0
+    coded = jnp.where(first, coded[: 2 * owners], coded[2 * owners :])
+    out_ref[:, :, 12 * LANES :] = cut(coded, 0)
     for copy in copies[3:]:
         copy.wait()
     weight = weight_ref[...].astype(f32)
@@ -189,22 +197,30 @@
     plan_ref[groups + 2 : groups + 3, :] = number.astype(i32)
     copy = pltpu.make_async_copy(plan_ref, plan, sem)
     copy.start()
-    sums_ref[...] = jnp.zeros_like(sums_ref)
+    def lay(row, values):
+        for half in range(2):
+            at = pl.ds(row + half, places, stride=DEEP)
+            sums_ref[at, :HALF] = values[:, half * HALF : (half + 1) * HALF]
+
+    for a in range(4):
+        cols = slice(a * LANES, (a + 1) * LANES)
+        old = weight_ref[:, cols]
+        lay(2 * a, old)
+        for c in range(4):
+            lay(8 * c + 8 + 2 * a, old * tsdf_ref[:, c, cols])
     copy.wait()
 
-    lanes = ids((LANES, LANES), 0).astype(f32).astype(bf16)
+    lanes = ids((HALF, LANES), 0).astype(f32).astype(bf16)
     sub = ids((8, LANES), 0)
+    level = sub.astype(f32)
     one, zero = jnp.ones((), bf16), jnp.zeros((), bf16)
 
     def halves(tiles, upper, lower, b):
-        hot = jnp.where(lanes == jnp.broadcast_to(lower[b : b + 1], (LANES, LANES)), one, zero)
-        feature = jnp.zeros((8, LANES), f32)
-        for c in range(5):
-            value = jnp.broadcast_to(tiles[1 + c][b : b + 1], (8, LANES))
-            feature = jnp.where(sub == c, value, feature)
-        level = jnp.broadcast_to(upper[b : b + 1], (8, LANES))
-        left = [jnp.where(level == a, feature, 0.0) for a in range(4)]
-        return hot, jnp.concatenate(left, axis=0).astype(bf16)
+        hot = jnp.where(lanes == jnp.broadcast_to(lower[b : b + 1], (HALF, LANES)), one, zero)
+        here = jnp.broadcast_to(upper[b : b + 1], (8, LANES)) == level
+        rows = [jnp.broadcast_to(tiles[1 + c][b : b + 1], (8, LANES)) for c in range(5)]
+        left = [jnp.where(here, row, 0.0) for row in rows]
+        return hot, jnp.concatenate(left, axis=0)
 
     def step(n, carry):
         for u in range(WIDE):
@@ -218,8 +234,8 @@
                 for c in range(6)
             ]
             voxel = tiles[0] + 256.0
-            upper = jnp.floor(voxel * (1.0 / LANES))
-            lower = (voxel - upper * float(LANES)).astype(bf16)
+            upper = jnp.floor(voxel * (1.0 / HALF))
+            lower = (voxel - upper * float(HALF)).astype(bf16)
             for b in range(0, UNIT, 2):
                 hot_a, left_a = halves(tiles, upper, lower, b)
                 hot_b, left_b = halves(tiles, upper, lower, b + 1)
@@ -230,30 +246,41 @@
                         jnp.concatenate([empty, left_b], axis=1),
                     ],
                     axis=0,
-                )
+                ).astype(bf16)
                 grids = dot(left, jnp.concatenate([hot_a, hot_b], axis=1), ((1,), (1,)))
                 for k in range(2):
-                    at = pl.multiple_of(plan[group, within + b + k] * 32, 32)
-                    sums_ref[pl.ds(at, 32), :] += grids[k * 32 : (k + 1) * 32]
+                    at = pl.multiple_of(plan[group, within + b + k] * DEEP, 8)
+                    sums_ref[pl.ds(at, DEEP), :HALF] += grids[k * DEEP : (k + 1) * DEEP]
         return carry
 
     lax.fori_loop(0, (plan[groups + 2, 0] + WIDE - 1) // WIDE, step, 0)
 
+    def taken(row):
+        halves = [sums_ref[pl.ds(row + half, PART, stride=DEEP), :HALF] for half in range(2)]
+        return jnp.concatenate(halves, axis=1)
+
     copies = []
-    for a in range(4):
-        cols = slice(a * LANES, (a + 1) * LANES)
-        old = weight_ref[:, cols]
-        new = old + sums_ref[pl.ds(a * 8, places, stride=32), :]
-        new_weight_ref[:, cols] = new
-        for c in range(4):
-            share = sums_ref[pl.ds(a * 8 + 1 + c, places, stride=32), :]
-            new_tsdf_ref[:, c, cols] = (old * tsdf_ref[:, c, cols] + share) / new
+    for first in range(0, places, PART):
+        part = slice(first, first + PART)
+        for a in range(4):
+            cols = slice(a * LANES, (a + 1) * LANES)
+            base = first * DEEP + 2 * a
+            new = taken(base)
+            new_weight_ref[part, cols] = new
+            scale = 1.0 / new
+            for c in range(4):
+                new_tsdf_ref[part, c, cols] = taken(base + 8 * c + 8) * scale
+        n = first // PART
         copies.append(
-            pltpu.make_async_copy(new_tsdf_ref.at[:, :, cols], new_tsdf_hbm.at[:, :, cols], sems.at[a])
+            pltpu.make_async_copy(new_tsdf_ref.at[part], new_tsdf_hbm.at[part], sems.at[2 * n])
         )
+        copies.append(
+            pltpu.make_async_copy(
+                new_weight_ref.at[part], new_weight_hbm.at[part], sems.at[2 * n + 1]
+            )
+        )
+        copies[-2].start()
         copies[-1].start()
-    copies.append(pltpu.make_async_copy(new_weight_ref, new_weight_hbm, sems.at[4]))
-    copies[-1].start()
     for copy in copies:
         copy.wait()
 
@@ -268,13 +295,13 @@
         ),
         out_specs=(pl.BlockSpec(memory_space=pl.ANY), pl.BlockSpec(memory_space=pl.ANY)),
         scratch_shapes=[
-            pltpu.VMEM(((places + 1) * 32, LANES), f32),
+            pltpu.VMEM(((places + 1) * DEEP, LANES), f32),
             pltpu.VMEM(old_tsdf.shape, f32),
             pltpu.VMEM(old_weight.shape, f32),
             pltpu.VMEM((8, LANES), i32),
             pltpu.SMEM((8, LANES), i32),
             pltpu.SemaphoreType.DMA(()),
-            pltpu.SemaphoreType.DMA((5,)),
+            pltpu.SemaphoreType.DMA((2 * places // PART,)),
         ],
         compiler_params=PARAMS,
         name="join",

time: 71.4 us -> 69.5 us (0.973)
  Pallas kernels: 10.4 us -> 8.49 us
    pallas_call x1, Pallas kernels: 6.92 us -> 5.21 us  [join(): pl.pallas_call(join_kernel, out_shape=(jax.ShapeDtypeStruct(old_tsdf.shap...]
where the time goes in v5:
time: 69.5 us; the launch traced here: 68.5 us
  blocking collectives  59.4 us (85%)
  Pallas kernels  8.49 us (12%)
    all_to_all x1, blocking collectives, local(): lax.all_to_all(packed, 'owner', split_axis=0, concat_axis=0, tiled=True)  44.9 us
    all_to_all x1, blocking collectives, local(): final = lax.all_to_all(sent, 'rep', split_axis=0, concat_axis=0, tiled=True)  14.4 us
    pallas_call x1, Pallas kernels, join(): pl.pallas_call(join_kernel, out_shape=(jax.ShapeDtypeStruct(old_tsdf.shap...  5.21 us
    pallas_call x1, Pallas kernels, pack(): pl.pallas_call(pack_kernel, out_shape=jax.ShapeDtypeStruct((counts.shape[...  2.2 us

profile of v5, /device:TPU:6, one launch (start us, length us, event | category | flops | bytes accessed | tf_op | source)
XLA Modules:
  0.0 68.5 jit_solution(14162452388216567335)
XLA Ops:
  0.6 2.2 %pack.1 = bf16[128,2,1664]{2,1,0:T(2,128)(2,1)S(1)} custom-call(s32[1,128]{1,0:T(1,128)} %refs_0_.1, s32[1,256]{1,0:T(1,128)} %bitcast.7, s32[256,128]{1,0:T(8,128)} %bitcast.6, s32[256,128]{1,0:T(8,128)} %refs_3_.1, bf16[256,128]{1,0:T(8,128)(2,1)} %refs_4_.1, bf16[256,128]{1,0:T(8,128)(2,1)} %refs_5_.1, bf16[3,256,128]{2,1,0:T(8,128)(2,1)} %bitcast.5), custom_call_target="tpu_custom_call" | custom-call | tf_op jit(solution)/shard_map/pack/pallas_call | solution.py:99
  2.8 44.9 %all_to_all.10.in_ref = bf16[128,2,1664]{2,1,0:T(2,128)(2,1)S(1)} all-to-all(bf16[128,2,1664]{2,1,0:T(2,128)(2,1)S(1)} %pack.1), channel_id=1, replica_groups=mesh['owner'=128,'rep'=4] {'owner'}, dimensions={0} | all-to-all | bytes 1703936 | tf_op jit(solution)/shard_map/all_to_all | solution.py:318
  47.8 1.1 %route.1 = bf16[4,136,768]{2,1,0:T(8,128)(2,1)S(1)} custom-call(bf16[128,2,1664]{2,1,0:T(2,128)(2,1)S(1)} %all_to_all.10.in_ref), custom_call_target="tpu_custom_call" | custom-call | tf_op jit(solution)/shard_map/route/pallas_call | solution.py:162
  48.9 0.0 copy-start
  48.9 0.0 copy-start.1
  48.9 14.4 %all_to_all.11 = bf16[4,136,768]{2,1,0:T(8,128)(2,1)S(1)} all-to-all(bf16[4,136,768]{2,1,0:T(8,128)(2,1)S(1)} %route.1), channel_id=1, replica_groups=mesh['owner'=128,'rep'=4] {'rep'}, dimensions={0} | all-to-all | bytes 1671168 | tf_op jit(solution)/shard_map/all_to_all | solution.py:320
  63.3 0.0 copy-done
  63.3 0.0 copy-done.1
  63.3 5.2 %join.1 = (f32[64,4,512]{2,1,0:T(4,128)}, f32[64,512]{1,0:T(8,128)}) custom-call(bf16[544,768]{1,0:T(8,128)(2,1)S(1)} %bitcast.4, f32[64,4,512]{2,1,0:T(4,128)S(1)} %copy-done, f32[64,512]{1,0:T(8,128)S(1)} %copy-done.1), custom_call_target="tpu_custom_call" | custom-call | tf_op jit(solution)/shard_map/join/pallas_call | solution.py:290
Async XLA Ops:
  48.9 14.4 %copy-start = (f32[64,4,512]{2,1,0:T(4,128)S(1)}, f32[64,4,512]{2,1,0:T(4,128)}, u32[]{:S(2)}) copy-start(f32[64,4,512]{2,1,0:T(4,128)} %tsdf_ref.1) | copy-start | bytes 1572868
  48.9 14.4 %copy-start.1 = (f32[64,512]{1,0:T(8,128)S(1)}, f32[64,512]{1,0:T(8,128)}, u32[]{:S(2)}) copy-start(f32[64,512]{1,0:T(8,128)} %weight_ref.1) | copy-start | bytes 393220
